TPU v7x, 256 devices: a whole 4x4x8 slice. The times are simulated.
256 devices in a mesh: dp: 64 (over y, z, x_lo), fsdp: 4 (over x_hi, core).
Axes of the slice: x: 4 (x_hi: 2, x_lo: 2; x = x_hi * 2 + x_lo), y: 4, z: 8, core: 2. Of those that a mesh axis runs over, the one named last changes fastest.
Arguments:
- picture_tower_inputs: bfloat16 [131072, 1152], P(('dp', 'fsdp')), may hold values from -6 to 6
- caption_tower_inputs: bfloat16 [131072, 1152], P(('dp', 'fsdp')), may hold values from -6 to 6
- halfwidth_parameter_matrix: bfloat16 [1152, 2304], P('fsdp'), may hold values from -0.1875 to 0.1875
- affinity_multiplier: float32 [1], replicated, may hold values from 4 to 12
- affinity_offset: float32 [1], replicated, may hold values from -6 to -2
- precise_parameter_copy: float32 [1152, 2304], P('fsdp', 'dp'), may hold values from -0.125 to 0.125
- gradient_mean_estimate: float32 [1152, 2304], P('fsdp', 'dp'), may hold values from -4 to 4
- gradient_variance_estimate: float32 [1152, 2304], P('fsdp', 'dp'), may hold values from 0.05 to 1
Outputs:
- img_tangent: bfloat16 [131072, 1152], P(('dp', 'fsdp'))
- txt_tangent: bfloat16 [131072, 1152], P(('dp', 'fsdp'))
- new_master: float32 [1152, 2304], P('fsdp', 'dp')
- new_one: float32 [1152, 2304], P('fsdp', 'dp')
- new_two: float32 [1152, 2304], P('fsdp', 'dp')
- new_weights: bfloat16 [1152, 2304], P('fsdp')
All inputs are finite; a program needn't handle non-finite values.
Results may differ from a plain program's by a relative error of at most 0.008.
Values may be sent and summed in bfloat16 or wider, within the bound.
No kernel may reach another device: no remote copies, remote signals or barrier semaphores. Data moves between devices by JAX's collectives and lax.ppermute only.
A program may use at most 128 MiB of HBM per device.

v0:
```python
import functools

import jax
import jax.numpy as jnp
from jax import lax
from jax.experimental import pallas as pl
from jax.experimental.pallas import tpu as pltpu
from jax.sharding import Mesh, PartitionSpec as P

PIECES = 2
LINE = ("y", "z")
AXES = ("y", "z", "xl", "xh", "c")
DP = ("y", "z", "xl")
FSDP = ("xh", "c")


def shifted(value, steps):
    count = lax.axis_size(LINE)
    return lax.ppermute(value, LINE, [(i, (i + steps) % count) for i in range(count)])


def swapped(value, axes):
    count = lax.axis_size(axes)
    return lax.ppermute(value, axes, [(i, count - 1 - i) for i in range(count)])


def gather_weights(own):
    across = swapped(own, ("xl", "xh"))
    beside = swapped(own, "c")
    far = swapped(across, "c")
    xh, c = lax.axis_index("xh"), lax.axis_index("c")
    rows = own.shape[0]
    tops = jnp.stack([2 * xh + c, 2 * xh + 1 - c, 2 - 2 * xh + c, 3 - 2 * xh - c]) * rows
    return tops.astype(jnp.int32), (own, beside, across, far)


def exchange(img, txt):
    even = lax.axis_index("xl") == 0
    two_t = shifted(txt, 1)
    two_i = shifted(img, -1)
    first = swapped(jnp.where(even, txt, img), "xl")
    one_t, one_i, three_t, three_i = [], [], [], []
    piece = txt.shape[0] // PIECES
    seconds = []
    for n in range(PIECES):
        cut = slice(n * piece, (n + 1) * piece)
        held = jnp.where(even, two_i[cut], two_t[cut])
        seconds.append(swapped(held, "xl"))
    for n in range(PIECES):
        cut = slice(n * piece, (n + 1) * piece)
        near, far = lax.optimization_barrier((first, seconds[n]))
        one_t.append(jnp.where(even, far, near[cut]))
        one_i.append(jnp.where(even, near[cut], far))
        three_t.append(shifted(one_t[n], 1))
        three_i.append(shifted(one_i[n], -1))
    return one_t, one_i, two_t, two_i, three_t, three_i


WIDTH = 1152
ROWS = 512
SHARE = 288
COLS = 36
FOLD = 3
TALL = SHARE // FOLD
LANES = 896
VMEM = pl.BlockSpec(memory_space=pltpu.VMEM)
SMEM = pl.BlockSpec(memory_space=pltpu.SMEM)


def dot(left, right, dims):
    return lax.dot_general(left, right, (dims, ((), ())), preferred_element_type=jnp.float32)


def project(rows, w):
    projected = dot(rows, w, ((1,), (0,)))
    norm = lax.rsqrt(jnp.sum(projected * projected, axis=-1, keepdims=True) + 1e-06)
    return projected * norm, norm


class Loads:
    def __init__(self, sems):
        self.sems, self.used = sems, 0

    def start(self, source, target):
        copy = pltpu.make_async_copy(source, target, self.sems.at[self.used])
        self.used += 1
        copy.start()
        return copy


def load_weights(loads, tops, shards, w, side):
    copies = []
    for n, shard in enumerate(shards):
        top = pl.multiple_of(tops[n], 32)
        source = shard.at[:, pl.ds(side * WIDTH, WIDTH)]
        copies.append(loads.start(source, w.at[side, pl.ds(top, SHARE), :]))
    return copies


def load_rows(loads, pieces, raw):
    rows = pieces[0].shape[0]
    return [loads.start(p, raw.at[pl.ds(n * rows, rows), :]) for n, p in enumerate(pieces)]


def wait(*groups):
    for group in groups:
        for copy in group:
            copy.wait()


def meet(raw, w, mine, mult, offset):
    other = project(raw, w)[0].astype(jnp.bfloat16)
    logits = mult * dot(mine[...], other, ((1,), (1,))) + offset
    weight = (jax.nn.sigmoid(logits) * mult).astype(jnp.bfloat16)
    return dot(weight, other, ((1,), (0,)))


def own_kernel(mult_ref, offset_ref, tops, *refs):
    shards, (img, txt), (unit, norm, low, acc, w, raw, sems) = refs[:4], refs[4:6], refs[6:]
    mult, offset = mult_ref[0], offset_ref[0]
    loads = Loads(sems)
    ready = []
    for side, rows in enumerate((img, txt)):
        ready.append(
            load_weights(loads, tops, shards, w, side) + load_rows(loads, [rows], raw.at[side])
        )

    def step(side, carry):
        for n in range(2):
            pl.when(side == n)(functools.partial(wait, ready[n]))
        u, inv = project(raw[side], w[side])
        unit[side] = u
        norm[side] = inv
        low[side] = u.astype(jnp.bfloat16)
        return carry

    lax.fori_loop(0, 2, step, 0)
    logits = mult * dot(low[0], low[1], ((1,), (1,))) + offset
    line = lax.broadcasted_iota(jnp.int32, logits.shape, 0)
    column = lax.broadcasted_iota(jnp.int32, logits.shape, 1)
    sign = jnp.where(line == column, 1.0, -1.0)
    pair = (-sign * jax.nn.sigmoid(-sign * logits) * mult).astype(jnp.bfloat16)
    acc[0] = dot(pair, low[1], ((1,), (0,)))
    acc[1] = dot(pair, low[0], ((0,), (0,)))


def meet_kernel(mult_ref, offset_ref, tops, *refs):
    shards, (two_t, two_i), refs = refs[:4], refs[4:6], refs[6:]
    texts, images, refs = refs[:PIECES], refs[PIECES : 2 * PIECES], refs[2 * PIECES :]
    in_low, in_acc, acc, w, raw, low, sems = refs
    mult, offset = mult_ref[0], offset_ref[0]
    loads = Loads(sems)
    ready = []
    for side, two in enumerate((two_t, two_i)):
        ready.append(
            load_weights(loads, tops, shards, w, 1 - side)
            + load_rows(loads, [two], raw.at[side])
            + [loads.start(in_low.at[side], low.at[side])]
            + [loads.start(in_acc.at[side], acc.at[side])]
        )
    for side, ones in enumerate((texts, images)):
        ready.append(load_rows(loads, ones, raw.at[2 + side]))

    def step(turn, carry):
        for n in range(4):
            pl.when(turn == n)(functools.partial(wait, ready[n]))
        side = lax.rem(turn, 2)
        acc[side] += meet(raw[turn], w[1 - side], low.at[side], mult, offset)
        return carry

    lax.fori_loop(0, 4, step, 0)


def tail_kernel(mult_ref, offset_ref, tops, *refs):
    shards, refs = refs[:4], refs[4:]
    texts, images, refs = refs[:PIECES], refs[PIECES : 2 * PIECES], refs[2 * PIECES :]
    in_low, in_acc, in_unit, in_norm, in_x, tan, chunks, w, raw, low, acc, unit, norm, x, sems = refs
    mult, offset = mult_ref[0], offset_ref[0]
    loads = Loads(sems)
    ready = []
    for side, rows in enumerate((texts, images)):
        ready.append(
            load_weights(loads, tops, shards, w, 1 - side)
            + load_rows(loads, rows, raw.at[side])
            + [loads.start(in_low.at[side], low.at[side])]
            + [loads.start(in_acc.at[side], acc.at[side])]
        )
    last = [loads.start(in_unit, unit), loads.start(in_norm, norm), loads.start(in_x, x)]

    def step(side, carry):
        for n in range(2):
            pl.when(side == n)(functools.partial(wait, ready[n]))
        acc[side] += meet(raw[side], w[1 - side], low.at[side], mult, offset)
        return carry

    lax.fori_loop(0, 2, step, 0)
    wait(last)

    def finish(n, carry):
        rows = pl.ds(pl.multiple_of(n * 64, 64), 64)
        for side in range(2):
            u, a = unit[side, rows, :], acc[side, rows, :]
            along = jnp.sum(u * a, axis=-1, keepdims=True)
            tan[side, rows, :] = (norm[side, rows, :] * (a - u * along)).astype(jnp.bfloat16)
        return carry

    lax.fori_loop(0, ROWS // 64, finish, 0)
    fill(chunks, tan, x)


def fill(chunks, tan, x):
    def step(t, carry):
        for xh in range(2):
            g = dot(tan[t], x[t, xh], ((0,), (0,)))
            for block in range(4):
                top = block * SHARE
                pieces = [g[top + q * TALL : top + (q + 1) * TALL] for q in range(FOLD)]
                pieces.append(jnp.zeros((TALL, LANES - FOLD * SHARE), jnp.float32))
                chunks[t * 8 + block * 2 + xh] = jnp.concatenate(pieces, axis=1).astype(
                    jnp.bfloat16
                )
        return carry

    lax.fori_loop(0, 2, step, 0)


def keep_kernel(tan, x, chunks):
    fill(chunks, tan, x)


def weave_kernel(parts, order, out):
    for half in range(2):
        stack = []
        for block in range(4):
            for q in range(FOLD):
                stack.append(parts[half * 4 + block, :, q * SHARE : (q + 1) * SHARE])
        total = dot(jnp.concatenate(stack, axis=0), order[...], ((0,), (0,)))
        out[:, half * WIDTH : (half + 1) * WIDTH] = total.astype(jnp.bfloat16)


def call(kernel, outs, args, flops, scalars=0, scratch=(), anywhere=False):
    moved = sum(a.size * a.dtype.itemsize for a in (*args, *outs))
    spec = pl.BlockSpec(memory_space=pl.ANY) if anywhere else VMEM
    copies = (pltpu.SemaphoreType.DMA((24,)),) if anywhere else ()
    return pl.pallas_call(
        kernel,
        out_shape=outs,
        in_specs=[SMEM] * scalars + [spec] * (len(args) - scalars),
        out_specs=[VMEM] * len(outs),
        scratch_shapes=(*scratch, *copies),
        cost_estimate=pl.CostEstimate(flops=flops, bytes_accessed=moved, transcendentals=0),
        compiler_params=pltpu.CompilerParams(vmem_limit_bytes=56 * 1024 * 1024),
    )(*args)


def shaped(shape, dtype):
    return jax.ShapeDtypeStruct(shape, dtype)


def column_order():
    p = lax.iota(jnp.int32, WIDTH)
    y, xl = p // 576, p % 576 // 288
    q, z, i = p % 288 // 96, p % 96 // 12, p % 12
    natural = ((y * 8 + z) * 2 + xl) * COLS + q * 12 + i
    return (natural[:, None] == lax.iota(jnp.int32, WIDTH)[None, :]).astype(jnp.bfloat16)


def inner(
    picture_tower_inputs,
    caption_tower_inputs,
    halfwidth_parameter_matrix,
    affinity_multiplier,
    affinity_offset,
    precise_parameter_copy,
    gradient_mean_estimate,
    gradient_variance_estimate,
):
    bf16, f32 = jnp.bfloat16, jnp.float32
    img, txt = picture_tower_inputs, caption_tower_inputs
    order = column_order()
    w = halfwidth_parameter_matrix
    w = jnp.concatenate(
        [
            dot(w[:, :WIDTH], order, ((1,), (1,))).astype(bf16),
            dot(w[:, WIDTH:], order, ((1,), (1,))).astype(bf16),
        ],
        axis=1,
    )
    tops, shards = gather_weights(w)
    scalars = (affinity_multiplier, affinity_offset, tops)

    one_t, one_i, two_t, two_i, three_t, three_i = exchange(img, txt)
    c = lax.axis_index("c")

    def columns(rows, core):
        parts = rows.reshape(ROWS, 2, 2, SHARE)
        return jnp.where(core == 0, parts[:, :, 0], parts[:, :, 1]).transpose(1, 0, 2)

    give_x = jnp.stack([columns(img, 1 - c), columns(txt, 1 - c)])
    keep_x = jnp.stack([columns(img, c), columns(txt, c)])

    def both(shape, dtype):
        return shaped((2, *shape), dtype), pltpu.VMEM((2, *shape), dtype)

    mac = 2 * ROWS * WIDTH
    big, vbig = both((ROWS, WIDTH), f32)
    flat, vflat = both((ROWS, 1), f32)
    low, vlow = both((ROWS, WIDTH), bf16)
    vw = pltpu.VMEM((2, WIDTH, WIDTH), bf16)
    unit_of, norm_of, low_of, acc = call(
        own_kernel,
        (big, flat, low, big),
        (*scalars, *shards, img, txt),
        mac * (2 * WIDTH + 3 * ROWS),
        scalars=3,
        scratch=(vw, vlow),
        anywhere=True,
    )
    (acc,) = call(
        meet_kernel,
        (big,),
        (*scalars, *shards, two_t, two_i, *one_t, *one_i, low_of, acc),
        mac * (4 * WIDTH + 8 * ROWS),
        scalars=3,
        scratch=(vw, pltpu.VMEM((4, ROWS, WIDTH), bf16), vlow),
        anywhere=True,
    )
    chunk = shaped((16, TALL, LANES), bf16)
    tan, give = call(
        tail_kernel,
        (low, chunk),
        (*scalars, *shards, *three_t, *three_i, low_of, acc, unit_of, norm_of, give_x),
        mac * (3 * WIDTH + 4 * ROWS),
        scalars=3,
        scratch=(vw, vlow, vlow, vbig, vbig, vflat, pltpu.VMEM((2, 2, ROWS, SHARE), bf16)),
        anywhere=True,
    )
    got = swapped(give, "c")
    (keep,) = call(keep_kernel, (chunk,), (tan, keep_x), mac * WIDTH)
    img_tangent = dot(tan[0], order, ((1,), (0,))).astype(bf16)
    txt_tangent = dot(tan[1], order, ((1,), (0,))).astype(bf16)

    chip = (keep.astype(f32) + got.astype(f32)).astype(bf16)
    parts = lax.all_to_all(chip, ("y", "xl", "xh"), 0, 0, tiled=True)
    plane = jnp.sum(parts.astype(f32), axis=0).astype(bf16)
    parts = lax.all_to_all(plane.reshape(8, 12, LANES), "z", 0, 0, tiled=True)
    gradient = jnp.sum(parts.astype(f32), axis=0)[:, : FOLD * SHARE]
    gradient = gradient.reshape(12, FOLD, SHARE).transpose(2, 1, 0).reshape(SHARE, COLS)

    new_one = 0.9 * gradient_mean_estimate + 0.1 * gradient
    new_two = 0.95 * gradient_variance_estimate + 0.05 * gradient * gradient
    new_master = precise_parameter_copy - 0.001 * (
        new_one / (jnp.sqrt(new_two) + 1e-08) + 0.1 * precise_parameter_copy
    )
    mine = new_master.astype(bf16).reshape(SHARE, FOLD, 12).transpose(2, 1, 0)
    mine = jnp.pad(mine.reshape(1, 12, FOLD * SHARE), ((0, 0), (0, 0), (0, LANES - FOLD * SHARE)))
    line = lax.all_to_all(jnp.broadcast_to(mine, (8, 12, LANES)), "z", 0, 0, tiled=True)
    line = jnp.broadcast_to(line.reshape(1, TALL, LANES), (8, TALL, LANES))
    parts = lax.all_to_all(line, ("y", "xl"), 0, 0, tiled=True)
    (new_weights,) = call(
        weave_kernel, (shaped((SHARE, 2 * WIDTH), bf16),), (parts, order), 4 * SHARE * WIDTH * WIDTH
    )
    return (img_tangent, txt_tangent, new_master, new_one, new_two, new_weights)


def solution(mesh):
    fine = Mesh(mesh.devices.reshape(4, 8, 2, 2, 2), AXES)
    rows = P(DP + FSDP, None)
    state = P(FSDP, DP)
    return jax.shard_map(
        inner,
        mesh=fine,
        in_specs=(rows, rows, P(FSDP, None), P(), P(), state, state, state),
        out_specs=(rows, rows, state, state, state, P(FSDP, None)),
        check_vma=False,
    )
```

profile of v0, /device:TPU:4, one launch (start us, length us, event | category | flops | bytes accessed | tf_op | source)
XLA Modules:
  0.0 242.6 jit_solution(11830308144751475087)
XLA Ops:
  0.6 8.4 %collective-permute-start.4 = (bf16[512,1152]{1,0:T(8,128)(2,1)}, bf16[512,1152]{1,0:T(8,128)(2,1)}, u32[]{:S(2)}, u32[]{:S(2)}) collective-permute-start(bf16[512,1152]{1,0:T(8,128)(2,1)} %refs_4_.1), channel_id=1, source_target_pairs={{0,248},{8,0},{16,8},{24,16},{32,24},{40,32},{48,40},{56,48},{64,5... | collective-permute-start | bytes 3538952 | tf_op jit(solution)/shard_map/ppermute | solution.py:19
  9.1 2.5 %fusion.13 = bf16[288,1152]{1,0:T(8,128)(2,1)S(1)} fusion(s32[1152]{0:T(1024)S(1)} %fusion.46, bf16[288,2304]{1,0:T(8,128)(2,1)} %param.10), kind=kOutput, calls=%fused_computation.15 | convolution fusion | flops 766070784 | bytes 1331712 | tf_op jit(solution)/shard_map/dot_general | solution.py:71
  11.6 1.3 fusion.14
  16.2 1.2 collective-permute-start.3
  20.8 1.4 copy.29
  23.9 1.4 copy.32
  25.3 9.2 %collective-permute-done.4.refs_5_ = bf16[512,1152]{1,0:T(8,128)(2,1)} collective-permute-done((bf16[512,1152]{1,0:T(8,128)(2,1)}, bf16[512,1152]{1,0:T(8,128)(2,1)}, u32[]{:S(2)}, u32[]{:S(2)}) %collective-permute-start.4) | collective-permute-done | bytes 1179680 | tf_op jit(solution)/shard_map/ppermute | solution.py:19
  34.6 5.5 %collective-permute-done.5.refs_4_ = bf16[512,1152]{1,0:T(8,128)(2,1)} collective-permute-done((bf16[512,1152]{1,0:T(8,128)(2,1)}, bf16[512,1152]{1,0:T(8,128)(2,1)}, u32[]{:S(2)}, u32[]{:S(2)}) %collective-permute-start.5) | collective-permute-done | bytes 1179680 | tf_op jit(solution)/shard_map/ppermute | solution.py:19
  40.1 1.7 slice_select_fusion
  41.8 1.3 collective-permute-start.8
  45.7 1.5 pad_maximum_fusion.refs_12_
  47.1 11.0 %collective-permute-done.8 = bf16[256,1152]{1,0:T(8,128)(2,1)S(1)} collective-permute-done((bf16[256,1152]{1,0:T(8,128)(2,1)S(1)}, bf16[256,1152]{1,0:T(8,128)(2,1)S(1)}, u32[]{:S(2)}, u32[]{:S(2)}) %collective-permute-start.8) | collective-permute-done | bytes 589856 | tf_op jit(solution)/shard_map/ppermute | solution.py:24
  58.1 11.6 %collective-permute-done.6 = bf16[256,1152]{1,0:T(8,128)(2,1)S(1)} collective-permute-done((bf16[256,1152]{1,0:T(8,128)(2,1)S(1)}, bf16[256,1152]{1,0:T(8,128)(2,1)S(1)}, u32[]{:S(2)}, u32[]{:S(2)}) %collective-permute-start.6) | collective-permute-done | bytes 589856 | tf_op jit(solution)/shard_map/ppermute | solution.py:24
  69.7 1.2 broadcast_select_fusion.2
  70.9 5.4 %collective-permute-start.10 = (bf16[256,1152]{1,0:T(8,128)(2,1)S(1)}, bf16[256,1152]{1,0:T(8,128)(2,1)S(1)}, u32[]{:S(2)}, u32[]{:S(2)}) collective-permute-start(bf16[256,1152]{1,0:T(8,128)(2,1)S(1)} %get-tuple-element.34.refs_8_), channel_id=1, source_target_pairs={{0,248},{8,0},{16,8},{24,16},{32,24},{40,32},{48,40},{56,48},{64,5... | collective-permute-start | bytes 1769480 | tf_op jit(solution)/shard_map/ppermute | solution.py:19
  78.1 1.7 collective-permute-start.7
  80.9 11.7 %shard_map.127 = (f32[2,512,1152]{2,1,0:T(8,128)}, f32[2,512,1]{2,1,0:T(8,128)}, bf16[2,512,1152]{2,1,0:T(8,128)(2,1)}, f32[2,512,1152]{2,1,0:T(8,128)}) custom-call(f32[1]{0:T(128)S(6)} %copy.35.mult_ref, f32[1]{0:T(128)S(6)} %copy.36.offset_ref, s32[4]{0:T(128)} %add_multiply_fusion.tops, bf16[288,2304]{1,0:T(8,128)(2,1)} %pad_maximum_fusion.2.refs_0_, ...), custom_call_target="tpu_custom_call" | custom-call | flops 4529848320 | bytes 19468312 | tf_op jit(solution)/shard_map/pallas_call | solution.py:245
  92.6 21.8 %shard_map.128.refs_9_ = f32[2,512,1152]{2,1,0:T(8,128)} custom-call(f32[1]{0:T(128)S(6)} %copy.35.mult_ref, f32[1]{0:T(128)S(6)} %copy.36.offset_ref, s32[4]{0:T(128)} %add_multiply_fusion.tops, bf16[288,2304]{1,0:T(8,128)(2,1)} %pad_maximum_fusion.2.refs_0_, bf16[288,2304]{1,0:T(8,128)(2,1)} %collective-permute-done.refs_1_, ...), custom_call_target="tpu_custom_call" | custom-call | flops 10267656192 | bytes 21823512 | tf_op jit(solution)/shard_map/pallas_call | solution.py:245
  115.9 17.9 %shard_map.129 = (bf16[2,512,1152]{2,1,0:T(8,128)(2,1)}, bf16[16,96,896]{2,1,0:T(8,128)(2,1)}) custom-call(f32[1]{0:T(128)S(6)} %copy.35.mult_ref, f32[1]{0:T(128)S(6)} %copy.36.offset_ref, s32[4]{0:T(128)} %add_multiply_fusion.tops, bf16[288,2304]{1,0:T(8,128)(2,1)} %pad_maximum_fusion.2.refs_0_, bf16[288,2304]{1,0:T(8,128)(2,1)} %collective-permute-done.refs_1_, ...), custom_call_target="tpu_custom_call" | custom-call | flops 6492782592 | bytes 25759768 | tf_op jit(solution)/shard_map/pallas_call | solution.py:245
  134.1 1.5 pad_maximum_fusion.1.x
  135.6 6.6 %shard_map.130 = bf16[16,96,896]{2,1,0:T(8,128)(2,1)} custom-call(bf16[2,512,1152]{2,1,0:T(8,128)(2,1)} %get-tuple-element.24.tan, bf16[2,2,512,288]{3,2,1,0:T(8,128)(2,1)} %pad_maximum_fusion.1.x), custom_call_target="tpu_custom_call" | custom-call | flops 1358954496 | bytes 6291456 | tf_op jit(solution)/shard_map/pallas_call | solution.py:245
  142.3 2.5 %add_convert_fusion = bf16[16,96,896]{2,1,0:T(8,128)(2,1)S(1)} fusion(bf16[16,96,896]{2,1,0:T(8,128)(2,1)S(1)} %collective-permute-done.12, bf16[16,96,896]{2,1,0:T(8,128)(2,1)} %shard_map.130), kind=kLoop, calls=%fused_computation | loop fusion | flops 5505024 | bytes 8257536 | tf_op jit(solution)/shard_map/convert_element_type | solution.py:343
  144.7 39.5 %all_to_all.20 = bf16[16,96,896]{2,1,0:T(8,128)(2,1)S(1)} all-to-all(bf16[16,96,896]{2,1,0:T(8,128)(2,1)S(1)} %add_convert_fusion), channel_id=1, replica_groups=mesh['y'=4,'z'=8,'xl'=2,'xh'=2,'c'=2] {'y','xl','xh'}, dimensions={0} | all-to-all | bytes 5505024 | tf_op jit(solution)/shard_map/all_to_all | solution.py:344
  184.7 16.2 %all_to_all.21 = bf16[8,12,896]{2,1,0:T(8,128)(2,1)S(1)} all-to-all(bf16[8,12,896]{2,1,0:T(8,128)(2,1)S(1)} %reshape.117), channel_id=1, replica_groups=mesh['y'=4,'z'=8,'xl'=2,'xh'=2,'c'=2] {'z'}, dimensions={0} | all-to-all | bytes 344064 | tf_op jit(solution)/shard_map/all_to_all | solution.py:346
  202.0 12.5 %all_to_all.22 = bf16[8,12,896]{2,1,0:T(8,128)(2,1)S(1)} all-to-all(bf16[8,12,896]{2,1,0:T(8,128)(2,1)S(1)} %broadcast_in_dim.17), channel_id=1, replica_groups=mesh['y'=4,'z'=8,'xl'=2,'xh'=2,'c'=2] {'z'}, dimensions={0} | all-to-all | bytes 344064 | tf_op jit(solution)/shard_map/all_to_all | solution.py:357
  214.6 1.2 broadcast_in_dim.19
  215.8 3.6 %all-to-all-start.3 = ((bf16[8,96,896]{2,1,0:T(8,128)(2,1)}), bf16[8,96,896]{2,1,0:T(8,128)(2,1)S(1)}, u32[]{:S(2)}, u32[]{:S(2)}) async-start(bf16[8,96,896]{2,1,0:T(8,128)(2,1)} %broadcast_in_dim.19), calls=%async_computation.3 | async-start | bytes 2752512 | tf_op jit(solution)/shard_map/all_to_all | solution.py:359
  219.3 2.0 fusion.order
  221.4 3.0 %fusion.6 = bf16[512,1152]{1,0:T(8,128)(2,1)} fusion(s32[1152]{0:T(1024)S(1)} %fusion.46, bf16[2,512,1152]{2,1,0:T(8,128)(2,1)S(1)} %copy-done.2), kind=kOutput, calls=%fused_computation.8 | convolution fusion | flops 1360871424 | bytes 2367488 | tf_op jit(solution)/shard_map/dot_general | solution.py:71
  224.5 3.0 %fusion.5 = bf16[512,1152]{1,0:T(8,128)(2,1)} fusion(s32[1152]{0:T(1024)S(1)} %fusion.46, bf16[2,512,1152]{2,1,0:T(8,128)(2,1)S(1)} %copy-done.2), kind=kOutput, calls=%fused_computation.7 | convolution fusion | flops 1360871424 | bytes 2367488 | tf_op jit(solution)/shard_map/dot_general | solution.py:71
  227.5 8.2 %all-to-all-done.3.parts = bf16[8,96,896]{2,1,0:T(8,128)(2,1)S(1)} async-done(((bf16[8,96,896]{2,1,0:T(8,128)(2,1)}), bf16[8,96,896]{2,1,0:T(8,128)(2,1)S(1)}, u32[]{:S(2)}, u32[]{:S(2)}) %all-to-all-start.3) | async-done | bytes 1376288 | tf_op jit(solution)/shard_map/all_to_all | solution.py:359
  236.8 5.7 %shard_map.131 = bf16[288,2304]{1,0:T(8,128)(2,1)} custom-call(bf16[8,96,896]{2,1,0:T(8,128)(2,1)} %copy-done.3, bf16[1152,1152]{1,0:T(8,128)(2,1)} %fusion.order), custom_call_target="tpu_custom_call" | custom-call | flops 1528823808 | bytes 5357568 | tf_op jit(solution)/shard_map/pallas_call | solution.py:245
  (76 shorter events, 16.9 us)
Async XLA Ops:
  0.6 33.9 %collective-permute-start.4 = (bf16[512,1152]{1,0:T(8,128)(2,1)}, bf16[512,1152]{1,0:T(8,128)(2,1)}, u32[]{:S(2)}, u32[]{:S(2)}) collective-permute-start(bf16[512,1152]{1,0:T(8,128)(2,1)} %refs_4_.1), channel_id=1, source_target_pairs={{0,248},{8,0},{16,8},{24,16},{32,24},{40,32},{48,40},{56,48},{64,5... | collective-permute-start | bytes 3538952 | tf_op jit(solution)/shard_map/ppermute | solution.py:19
  9.0 31.1 %collective-permute-start.5 = (bf16[512,1152]{1,0:T(8,128)(2,1)}, bf16[512,1152]{1,0:T(8,128)(2,1)}, u32[]{:S(2)}, u32[]{:S(2)}) collective-permute-start(bf16[512,1152]{1,0:T(8,128)(2,1)} %refs_5_.1), channel_id=1, source_target_pairs={{0,8},{8,16},{16,24},{24,32},{32,40},{40,48},{48,56},{56,64},{64,7... | collective-permute-start | bytes 3538952 | tf_op jit(solution)/shard_map/ppermute | solution.py:19
  9.1 2.5 %copy-start.11 = (bf16[288,2304]{1,0:T(8,128)(2,1)S(1)}, bf16[288,2304]{1,0:T(8,128)(2,1)}, u32[]{:S(2)}) copy-start(bf16[288,2304]{1,0:T(8,128)(2,1)} %param.10) | copy-start | bytes 3981316
  12.9 1.8 copy-start
  12.9 2.1 copy-start.1
  14.1 30.9 %collective-permute-start.1 = (bf16[288,2304]{1,0:T(8,128)(2,1)}, bf16[288,2304]{1,0:T(8,128)(2,1)}, u32[]{:S(2)}, u32[]{:S(2)}) collective-permute-start(bf16[288,2304]{1,0:T(8,128)(2,1)} %pad_maximum_fusion.2.refs_0_), channel_id=1, source_target_pairs={{0,6},{2,4},{4,2},{6,0},{1,7},{3,5},{5,3},{7,1},{8,14},{10,12},{12... | collective-permute-start | bytes 3981320 | tf_op jit(solution)/shard_map/ppermute | solution.py:24
  14.6 65.1 %collective-permute-start = (bf16[288,2304]{1,0:T(8,128)(2,1)}, bf16[288,2304]{1,0:T(8,128)(2,1)}, u32[]{:S(2)}, u32[]{:S(2)}) collective-permute-start(bf16[288,2304]{1,0:T(8,128)(2,1)} %pad_maximum_fusion.2.refs_0_), channel_id=1, source_target_pairs={{0,1},{1,0},{2,3},{3,2},{4,5},{5,4},{6,7},{7,6},{8,9},{9,8},{10,11... | collective-permute-start | bytes 3981320 | tf_op jit(solution)/shard_map/ppermute | solution.py:24
  16.2 31.0 %collective-permute-start.3 = (bf16[512,1152]{1,0:T(8,128)(2,1)}, bf16[512,1152]{1,0:T(8,128)(2,1)}, u32[]{:S(2)}, u32[]{:S(2)}) collective-permute-start(bf16[512,1152]{1,0:T(8,128)(2,1)} %broadcast_select_fusion), channel_id=1, source_target_pairs={{0,4},{4,0},{1,5},{5,1},{2,6},{6,2},{3,7},{7,3},{8,12},{12,8},{9,1... | collective-permute-start | bytes 3538952 | tf_op jit(solution)/shard_map/ppermute | solution.py:24
  41.8 16.3 %collective-permute-start.8 = (bf16[256,1152]{1,0:T(8,128)(2,1)S(1)}, bf16[256,1152]{1,0:T(8,128)(2,1)S(1)}, u32[]{:S(2)}, u32[]{:S(2)}) collective-permute-start(bf16[256,1152]{1,0:T(8,128)(2,1)S(1)} %get-tuple-element.30), channel_id=1, source_target_pairs={{0,4},{4,0},{1,5},{5,1},{2,6},{6,2},{3,7},{7,3},{8,12},{12,8},{9,1... | collective-permute-start | bytes 1769480 | tf_op jit(solution)/shard_map/ppermute | solution.py:24
  43.1 26.6 %collective-permute-start.6 = (bf16[256,1152]{1,0:T(8,128)(2,1)S(1)}, bf16[256,1152]{1,0:T(8,128)(2,1)S(1)}, u32[]{:S(2)}, u32[]{:S(2)}) collective-permute-start(bf16[256,1152]{1,0:T(8,128)(2,1)S(1)} %get-tuple-element.31), channel_id=1, source_target_pairs={{0,4},{4,0},{1,5},{5,1},{2,6},{6,2},{3,7},{7,3},{8,12},{12,8},{9,1... | collective-permute-start | bytes 1769480 | tf_op jit(solution)/shard_map/ppermute | solution.py:24
  45.0 34.8 %collective-permute-start.2 = (bf16[288,2304]{1,0:T(8,128)(2,1)}, bf16[288,2304]{1,0:T(8,128)(2,1)S(1)}, u32[]{:S(2)}, u32[]{:S(2)}) collective-permute-start(bf16[288,2304]{1,0:T(8,128)(2,1)} %collective-permute-done.1.refs_2_), channel_id=1, source_target_pairs={{0,1},{1,0},{2,3},{3,2},{4,5},{5,4},{6,7},{7,6},{8,9},{9,8},{10,11... | collective-permute-start | bytes 3981320 | tf_op jit(solution)/shard_map/ppermute | solution.py:24
  70.8 21.8 %copy-start.4 = (bf16[256,1152]{1,0:T(8,128)(2,1)}, bf16[256,1152]{1,0:T(8,128)(2,1)S(1)}, u32[]{:S(2)}) copy-start(bf16[256,1152]{1,0:T(8,128)(2,1)S(1)} %get-tuple-element.35.refs_6_) | copy-start | bytes 1769476
  70.9 21.8 %copy-start.6 = (bf16[256,1152]{1,0:T(8,128)(2,1)}, bf16[256,1152]{1,0:T(8,128)(2,1)S(1)}, u32[]{:S(2)}) copy-start(bf16[256,1152]{1,0:T(8,128)(2,1)S(1)} %get-tuple-element.34.refs_8_) | copy-start | bytes 1769476
  70.9 43.6 %collective-permute-start.10 = (bf16[256,1152]{1,0:T(8,128)(2,1)S(1)}, bf16[256,1152]{1,0:T(8,128)(2,1)S(1)}, u32[]{:S(2)}, u32[]{:S(2)}) collective-permute-start(bf16[256,1152]{1,0:T(8,128)(2,1)S(1)} %get-tuple-element.34.refs_8_), channel_id=1, source_target_pairs={{0,248},{8,0},{16,8},{24,16},{32,24},{40,32},{48,40},{56,48},{64,5... | collective-permute-start | bytes 1769480 | tf_op jit(solution)/shard_map/ppermute | solution.py:19
  77.5 15.2 %copy-start.5 = (bf16[256,1152]{1,0:T(8,128)(2,1)}, bf16[256,1152]{1,0:T(8,128)(2,1)S(1)}, u32[]{:S(2)}) copy-start(bf16[256,1152]{1,0:T(8,128)(2,1)S(1)} %get-tuple-element.33.refs_7_) | copy-start | bytes 1769476
  77.5 15.2 %copy-start.7 = (bf16[256,1152]{1,0:T(8,128)(2,1)}, bf16[256,1152]{1,0:T(8,128)(2,1)S(1)}, u32[]{:S(2)}) copy-start(bf16[256,1152]{1,0:T(8,128)(2,1)S(1)} %get-tuple-element.32.refs_9_) | copy-start | bytes 1769476
  77.5 37.0 %collective-permute-start.11 = (bf16[256,1152]{1,0:T(8,128)(2,1)S(1)}, bf16[256,1152]{1,0:T(8,128)(2,1)S(1)}, u32[]{:S(2)}, u32[]{:S(2)}) collective-permute-start(bf16[256,1152]{1,0:T(8,128)(2,1)S(1)} %get-tuple-element.32.refs_9_), channel_id=1, source_target_pairs={{0,248},{8,0},{16,8},{24,16},{32,24},{40,32},{48,40},{56,48},{64,5... | collective-permute-start | bytes 1769480 | tf_op jit(solution)/shard_map/ppermute | solution.py:19
  78.1 36.4 %collective-permute-start.7 = (bf16[256,1152]{1,0:T(8,128)(2,1)S(1)}, bf16[256,1152]{1,0:T(8,128)(2,1)S(1)}, u32[]{:S(2)}, u32[]{:S(2)}) collective-permute-start(bf16[256,1152]{1,0:T(8,128)(2,1)S(1)} %get-tuple-element.35.refs_6_), channel_id=1, source_target_pairs={{0,8},{8,16},{16,24},{24,32},{32,40},{40,48},{48,56},{56,64},{64,7... | collective-permute-start | bytes 1769480 | tf_op jit(solution)/shard_map/ppermute | solution.py:19
  79.8 34.8 %collective-permute-start.9 = (bf16[256,1152]{1,0:T(8,128)(2,1)S(1)}, bf16[256,1152]{1,0:T(8,128)(2,1)S(1)}, u32[]{:S(2)}, u32[]{:S(2)}) collective-permute-start(bf16[256,1152]{1,0:T(8,128)(2,1)S(1)} %get-tuple-element.33.refs_7_), channel_id=1, source_target_pairs={{0,8},{8,16},{16,24},{24,32},{32,40},{40,48},{48,56},{56,64},{64,7... | collective-permute-start | bytes 1769480 | tf_op jit(solution)/shard_map/ppermute | solution.py:19
  79.8 1.1 copy-start.12
  114.5 0.8 copy-start.13
  114.5 1.0 copy-start.14
  114.5 1.2 copy-start.15
  114.5 1.3 copy-start.16
  133.8 8.5 %collective-permute-start.12 = (bf16[16,96,896]{2,1,0:T(8,128)(2,1)}, bf16[16,96,896]{2,1,0:T(8,128)(2,1)S(1)}, u32[]{:S(2)}, u32[]{:S(2)}) collective-permute-start(bf16[16,96,896]{2,1,0:T(8,128)(2,1)} %get-tuple-element.25), channel_id=1, source_target_pairs={{0,1},{1,0},{2,3},{3,2},{4,5},{5,4},{6,7},{7,6},{8,9},{9,8},{10,11... | collective-permute-start | bytes 8257544 | tf_op jit(solution)/shard_map/ppermute | solution.py:24
  184.7 16.4 %copy-start.8 = (f32[288,36]{0,1:T(8,128)S(1)}, f32[288,36]{0,1:T(8,128)}, u32[]{:S(2)}) copy-start(f32[288,36]{0,1:T(8,128)} %param.13) | copy-start | bytes 124420
  184.7 16.4 %copy-start.9 = (f32[288,36]{0,1:T(8,128)S(1)}, f32[288,36]{0,1:T(8,128)}, u32[]{:S(2)}) copy-start(f32[288,36]{0,1:T(8,128)} %param.15) | copy-start | bytes 124420
  184.7 16.4 %copy-start.10 = (f32[288,36]{0,1:T(8,128)S(1)}, f32[288,36]{0,1:T(8,128)}, u32[]{:S(2)}) copy-start(f32[288,36]{0,1:T(8,128)} %param.14) | copy-start | bytes 124420
  215.8 20.0 %all-to-all-start.3 = ((bf16[8,96,896]{2,1,0:T(8,128)(2,1)}), bf16[8,96,896]{2,1,0:T(8,128)(2,1)S(1)}, u32[]{:S(2)}, u32[]{:S(2)}) async-start(bf16[8,96,896]{2,1,0:T(8,128)(2,1)} %broadcast_in_dim.19), calls=%async_computation.3 | async-start | bytes 2752512 | tf_op jit(solution)/shard_map/all_to_all | solution.py:359
  219.3 2.1 copy-start.2
  235.7 1.1 copy-start.3
where the time goes:
time: 243 us
  blocking collectives  68.2 us (28%)
  Pallas kernels  63.8 us (26%)
  waiting for transfers between devices  46.3 us (19%)
  starting transfers between devices  23.9 us (10%)
  other arithmetic  16 us (7%)
  local copies, waits for them, and re-layouts  12.2 us (5%)
  matrix products  9.91 us (4%)
    pallas_call x5, Pallas kernels, call(): pl.pallas_call(kernel, out_shape=outs, in_specs=[SMEM] * scalars + [spec]...  63.8 us
    all_to_all x1, blocking collectives, inner(): parts = lax.all_to_all(chip, ('y', 'xl', 'xh'), 0, 0, tiled=True)  39.5 us
    ppermute x7, waiting for transfers between devices, swapped(): return lax.ppermute(value, axes, [(i, count - 1 - i) for i in range(count)])  23.3 us
    all_to_all x1, blocking collectives, inner(): parts = lax.all_to_all(plane.reshape(8, 12, LANES), 'z', 0, 0, tiled=True)  16.2 us
    ppermute x6, starting transfers between devices, shifted(): lax.ppermute(value, LINE, [(i, (i + steps) % count) for i in range(count)])  16.1 us
    ppermute x6, waiting for transfers between devices, shifted(): lax.ppermute(value, LINE, [(i, (i + steps) % count) for i in range(count)])  14.7 us
    all_to_all x1, blocking collectives, inner(): lax.all_to_all(jnp.broadcast_to(mine, (8, 12, LANES)), 'z', 0, 0, tiled=T...  12.5 us
    dot_general x4, matrix products, dot(): lax.dot_general(left, right, (dims, ((), ())), preferred_element_type=jnp...  9.91 us
  transfers between devices with their start and end apart: 14, of which 6 were waited for; matrix products, arithmetic and copies ran while one was open for 12% of the time, Pallas kernels for 17%

commit v1 on v0

--- a/solution.py
+++ b/solution.py
@@ -24,12 +24,13 @@
     return lax.ppermute(value, axes, [(i, count - 1 - i) for i in range(count)])
 
 
-def gather_weights(own):
-    across = swapped(own, ("xl", "xh"))
+def gather_weights(raw, arrange):
+    across = arrange(swapped(raw, ("xl", "xh")))
+    own = arrange(raw)
     beside = swapped(own, "c")
     far = swapped(across, "c")
     xh, c = lax.axis_index("xh"), lax.axis_index("c")
-    rows = own.shape[0]
+    rows = raw.shape[0]
     tops = jnp.stack([2 * xh + c, 2 * xh + 1 - c, 2 - 2 * xh + c, 3 - 2 * xh - c]) * rows
     return tops.astype(jnp.int32), (own, beside, across, far)
 
@@ -92,7 +93,7 @@
     copies = []
     for n, shard in enumerate(shards):
         top = pl.multiple_of(tops[n], 32)
-        source = shard.at[:, pl.ds(side * WIDTH, WIDTH)]
+        source = shard.at[pl.ds(side * SHARE, SHARE), :]
         copies.append(loads.start(source, w.at[side, pl.ds(top, SHARE), :]))
     return copies
 
@@ -208,37 +209,48 @@
     fill(chunks, tan, x)
 
 
-def fill(chunks, tan, x):
-    def step(t, carry):
-        for xh in range(2):
-            g = dot(tan[t], x[t, xh], ((0,), (0,)))
-            for block in range(4):
-                top = block * SHARE
-                pieces = [g[top + q * TALL : top + (q + 1) * TALL] for q in range(FOLD)]
-                pieces.append(jnp.zeros((TALL, LANES - FOLD * SHARE), jnp.float32))
-                chunks[t * 8 + block * 2 + xh] = jnp.concatenate(pieces, axis=1).astype(
-                    jnp.bfloat16
-                )
+def fill(chunks, tan, x, ready=()):
+    def step(turn, carry):
+        for n, copies in enumerate(ready):
+            pl.when(turn == 2 * n)(functools.partial(wait, copies))
+        t, xh = turn // 2, lax.rem(turn, 2)
+        g = dot(tan[t], x[t, xh], ((0,), (0,)))
+        for block in range(4):
+            top = block * SHARE
+            pieces = [g[top + q * TALL : top + (q + 1) * TALL] for q in range(FOLD)]
+            pieces.append(jnp.zeros((TALL, LANES - FOLD * SHARE), jnp.float32))
+            whole = jnp.concatenate(pieces, axis=1).astype(jnp.bfloat16)
+            chunks[t * 8 + block * 2 + xh] = whole
+        return carry
+
+    lax.fori_loop(0, 4, step, 0)
+
+
+def keep_kernel(in_tan, in_i, in_t, chunks, tan, x, sems):
+    loads = Loads(sems)
+    ready = []
+    for side, source in enumerate((in_i, in_t)):
+        ready.append([loads.start(source, x.at[side]), loads.start(in_tan.at[side], tan.at[side])])
+    fill(chunks, tan, x, ready)
+
+
+def weave_kernel(parts, order, out):
+    def step(n, carry):
+        pieces = []
+        for y in range(2):
+            stack = []
+            for block in range(2):
+                for q in range(FOLD):
+                    stack.append(parts[n * 4 + y * 2 + block, :, q * SHARE : (q + 1) * SHARE])
+            pieces.append(dot(jnp.concatenate(stack, axis=0), order[...], ((0,), (0,))))
+        lanes = pl.ds(pl.multiple_of(n * WIDTH, 128), WIDTH)
+        out[:, lanes] = jnp.concatenate(pieces, axis=1).astype(jnp.bfloat16)
         return carry
 
     lax.fori_loop(0, 2, step, 0)
 
 
-def keep_kernel(tan, x, chunks):
-    fill(chunks, tan, x)
-
-
-def weave_kernel(parts, order, out):
-    for half in range(2):
-        stack = []
-        for block in range(4):
-            for q in range(FOLD):
-                stack.append(parts[half * 4 + block, :, q * SHARE : (q + 1) * SHARE])
-        total = dot(jnp.concatenate(stack, axis=0), order[...], ((0,), (0,)))
-        out[:, half * WIDTH : (half + 1) * WIDTH] = total.astype(jnp.bfloat16)
-
-
-def call(kernel, outs, args, flops, scalars=0, scratch=(), anywhere=False):
+def call(kernel, outs, args, flops, scalars=0, scratch=(), anywhere=False, limit=56):
     moved = sum(a.size * a.dtype.itemsize for a in (*args, *outs))
     spec = pl.BlockSpec(memory_space=pl.ANY) if anywhere else VMEM
     copies = (pltpu.SemaphoreType.DMA((24,)),) if anywhere else ()
@@ -249,7 +261,7 @@
         out_specs=[VMEM] * len(outs),
         scratch_shapes=(*scratch, *copies),
         cost_estimate=pl.CostEstimate(flops=flops, bytes_accessed=moved, transcendentals=0),
-        compiler_params=pltpu.CompilerParams(vmem_limit_bytes=56 * 1024 * 1024),
+        compiler_params=pltpu.CompilerParams(vmem_limit_bytes=limit * 1024 * 1024),
     )(*args)
 
 
@@ -257,12 +269,12 @@
     return jax.ShapeDtypeStruct(shape, dtype)
 
 
-def column_order():
-    p = lax.iota(jnp.int32, WIDTH)
+def column_order(width):
+    p = lax.iota(jnp.int32, width)
     y, xl = p // 576, p % 576 // 288
     q, z, i = p % 288 // 96, p % 96 // 12, p % 12
     natural = ((y * 8 + z) * 2 + xl) * COLS + q * 12 + i
-    return (natural[:, None] == lax.iota(jnp.int32, WIDTH)[None, :]).astype(jnp.bfloat16)
+    return (natural[:, None] == lax.iota(jnp.int32, width)[None, :]).astype(jnp.bfloat16)
 
 
 def inner(
@@ -277,18 +289,14 @@
 ):
     bf16, f32 = jnp.bfloat16, jnp.float32
     img, txt = picture_tower_inputs, caption_tower_inputs
-    order = column_order()
-    w = halfwidth_parameter_matrix
-    w = jnp.concatenate(
-        [
-            dot(w[:, :WIDTH], order, ((1,), (1,))).astype(bf16),
-            dot(w[:, WIDTH:], order, ((1,), (1,))).astype(bf16),
-        ],
-        axis=1,
-    )
-    tops, shards = gather_weights(w)
+    order = column_order(WIDTH)
+
+    def arrange(w):
+        sides = jnp.concatenate([w[:, :WIDTH], w[:, WIDTH:]], axis=0)
+        return dot(sides, order, ((1,), (1,))).astype(bf16)
+
+    tops, shards = gather_weights(halfwidth_parameter_matrix, arrange)
     scalars = (affinity_multiplier, affinity_offset, tops)
-
     one_t, one_i, two_t, two_i, three_t, three_i = exchange(img, txt)
     c = lax.axis_index("c")
 
@@ -297,7 +305,7 @@
         return jnp.where(core == 0, parts[:, :, 0], parts[:, :, 1]).transpose(1, 0, 2)
 
     give_x = jnp.stack([columns(img, 1 - c), columns(txt, 1 - c)])
-    keep_x = jnp.stack([columns(img, c), columns(txt, c)])
+    keep_i, keep_t = columns(img, c), columns(txt, c)
 
     def both(shape, dtype):
         return shaped((2, *shape), dtype), pltpu.VMEM((2, *shape), dtype)
@@ -336,7 +344,14 @@
         anywhere=True,
     )
     got = swapped(give, "c")
-    (keep,) = call(keep_kernel, (chunk,), (tan, keep_x), mac * WIDTH)
+    (keep,) = call(
+        keep_kernel,
+        (chunk,),
+        (tan, keep_i, keep_t),
+        mac * WIDTH,
+        scratch=(vlow, pltpu.VMEM((2, 2, ROWS, SHARE), bf16)),
+        anywhere=True,
+    )
     img_tangent = dot(tan[0], order, ((1,), (0,))).astype(bf16)
     txt_tangent = dot(tan[1], order, ((1,), (0,))).astype(bf16)
 
@@ -358,7 +373,11 @@
     line = jnp.broadcast_to(line.reshape(1, TALL, LANES), (8, TALL, LANES))
     parts = lax.all_to_all(line, ("y", "xl"), 0, 0, tiled=True)
     (new_weights,) = call(
-        weave_kernel, (shaped((SHARE, 2 * WIDTH), bf16),), (parts, order), 4 * SHARE * WIDTH * WIDTH
+        weave_kernel,
+        (shaped((SHARE, 2 * WIDTH), bf16),),
+        (parts, column_order(WIDTH // 2)),
+        2 * SHARE * WIDTH * WIDTH,
+        limit=16,
     )
     return (img_tangent, txt_tangent, new_master, new_one, new_two, new_weights)
 

time: 243 us -> 240 us (0.988)
  local copies, waits for them, and re-layouts: 12.2 us -> 19.5 us
  waiting for transfers between devices: 46.3 us -> 39 us
  matrix products: 9.91 us -> 13 us
    ppermute x7, waiting for transfers between devices: 23.3 us -> 19.2 us  [swapped(): return lax.ppermute(value, axes, [(i, count - 1 - i) for i in range(count)])]
    unnamed x40 -> x38, local copies, waits for them, and re-layouts: 8.81 us -> 12.9 us
    ppermute x6, waiting for transfers between devices: 14.7 us -> 11.1 us  [shifted(): lax.ppermute(value, LINE, [(i, (i + steps) % count) for i in range(count)])]
    ppermute x6, starting transfers between devices: 16.1 us -> 12.5 us  [shifted(): lax.ppermute(value, LINE, [(i, (i + steps) % count) for i in range(count)])]
    dot_general x4, matrix products: 9.91 us -> 13 us  [dot(): lax.dot_general(left, right, (dims, ((), ())), preferred_element_type=jnp...]
    transpose x0 -> x1, other arithmetic: none -> 2.88 us  [columns(): jnp.where(core == 0, parts[:, :, 0], parts[:, :, 1]).transpose(1, 0, 2)]
    slice x0 -> x2, local copies, waits for them, and re-layouts: none -> 2.79 us  [arrange(): sides = jnp.concatenate([w[:, :WIDTH], w[:, WIDTH:]], axis=0)]
  transfers between devices with their start and end apart: 14 -> 14, of which waited for: 6 -> 5; matrix products, arithmetic and copies ran while one was open for 12% -> 16% of each run, Pallas kernels for 17% -> 17%
where the time goes in v1:
time: 240 us; the launch traced here: 239 us
  blocking collectives  67 us (28%)
  Pallas kernels  62.9 us (26%)
  waiting for transfers between devices  39 us (16%)
  starting transfers between devices  21.6 us (9%)
  local copies, waits for them, and re-layouts  19.5 us (8%)
  other arithmetic  14.2 us (6%)
  matrix products  13 us (5%)
    pallas_call x5, Pallas kernels, call(): pl.pallas_call(kernel, out_shape=outs, in_specs=[SMEM] * scalars + [spec]...  62.9 us
    all_to_all x1, blocking collectives, inner(): parts = lax.all_to_all(chip, ('y', 'xl', 'xh'), 0, 0, tiled=True)  39.7 us
    ppermute x7, waiting for transfers between devices, swapped(): return lax.ppermute(value, axes, [(i, count - 1 - i) for i in range(count)])  19.2 us
    all_to_all x1, blocking collectives, inner(): parts = lax.all_to_all(plane.reshape(8, 12, LANES), 'z', 0, 0, tiled=True)  14.7 us
    dot_general x4, matrix products, dot(): lax.dot_general(left, right, (dims, ((), ())), preferred_element_type=jnp...  13 us
    unnamed x38, local copies, waits for them, and re-layouts  12.9 us
    all_to_all x1, blocking collectives, inner(): lax.all_to_all(jnp.broadcast_to(mine, (8, 12, LANES)), 'z', 0, 0, tiled=T...  12.5 us
    ppermute x6, starting transfers between devices, shifted(): lax.ppermute(value, LINE, [(i, (i + steps) % count) for i in range(count)])  12.5 us
  transfers between devices with their start and end apart: 14, of which 5 were waited for; matrix products, arithmetic and copies ran while one was open for 16% of the time, Pallas kernels for 17%

profile of v1, /device:TPU:4, one launch (start us, length us, event | category | flops | bytes accessed | tf_op | source)
XLA Modules:
  0.0 239.4 jit_solution(4269623227796292319)
XLA Ops:
  1.3 1.4 fusion.115
  2.7 3.3 %fusion.4.refs_0_ = bf16[576,1152]{1,0:T(8,128)(2,1)} fusion(s32[1152]{0:T(1024)S(1)} %fusion.60, bf16[288,1152]{1,0:T(8,128)(2,1)S(1)} %get-tuple-element.43, bf16[288,1152]{1,0:T(8,128)(2,1)S(1)} %get-tuple-element.42), kind=kOutput, calls=%fused_computation.6 | convolution fusion | flops 1533468672 | bytes 2658816 | tf_op jit(solution)/shard_map/dot_general | solution.py:72
  6.0 8.3 %collective-permute-start.4 = (bf16[512,1152]{1,0:T(8,128)(2,1)}, bf16[512,1152]{1,0:T(8,128)(2,1)}, u32[]{:S(2)}, u32[]{:S(2)}) collective-permute-start(bf16[512,1152]{1,0:T(8,128)(2,1)} %refs_4_.1), channel_id=1, source_target_pairs={{0,248},{8,0},{16,8},{24,16},{32,24},{40,32},{48,40},{56,48},{64,5... | collective-permute-start | bytes 3538952 | tf_op jit(solution)/shard_map/ppermute | solution.py:19
  15.4 2.4 %collective-permute-start.3 = (bf16[512,1152]{1,0:T(8,128)(2,1)}, bf16[512,1152]{1,0:T(8,128)(2,1)}, u32[]{:S(2)}, u32[]{:S(2)}) collective-permute-start(bf16[512,1152]{1,0:T(8,128)(2,1)} %broadcast_select_fusion), channel_id=1, source_target_pairs={{0,4},{4,0},{1,5},{5,1},{2,6},{6,2},{3,7},{7,3},{8,12},{12,8},{9,1... | collective-permute-start | bytes 3538952 | tf_op jit(solution)/shard_map/ppermute | solution.py:24
  17.9 1.6 copy.21
  22.5 1.4 copy.29
  23.9 2.2 copy.30
  27.3 2.3 copy.31
  29.5 2.3 copy.32
  31.8 2.9 %select_bitcast_fusion = (bf16[2,512,288]{2,1,0:T(8,128)(2,1)}, bf16[1,2,512,288]{3,2,1,0:T(8,128)(2,1)S(1)}, bf16[1,2,512,288]{3,2,1,0:T(8,128)(2,1)S(1)}, bf16[2,512,288]{2,1,0:T(8,128)(2,1)}) fusion(bf16[512,2,1,288]{3,0,1,2:T(8,128)(2,1)} %copy.31, bf16[512,2,1,288]{3,0,1,2:T(8,128)(2,1)} %copy.32, pred[]{:T(512)S(6)} %eq.70, pred[]{:T(512)S(6)} %eq.69, ...), kind=kLoop, calls=%fused_computation.28 | loop fusion | flops 1179648 | bytes 4718594 | tf_op jit(solution)/shard_map/transpose | solution.py:305
  34.7 5.8 %collective-permute-done.4.refs_5_ = bf16[512,1152]{1,0:T(8,128)(2,1)} collective-permute-done((bf16[512,1152]{1,0:T(8,128)(2,1)}, bf16[512,1152]{1,0:T(8,128)(2,1)}, u32[]{:S(2)}, u32[]{:S(2)}) %collective-permute-start.4) | collective-permute-done | bytes 1179680 | tf_op jit(solution)/shard_map/ppermute | solution.py:19
  40.5 5.3 %collective-permute-done.5.refs_4_ = bf16[512,1152]{1,0:T(8,128)(2,1)} collective-permute-done((bf16[512,1152]{1,0:T(8,128)(2,1)S(1)}, bf16[512,1152]{1,0:T(8,128)(2,1)}, u32[]{:S(2)}, u32[]{:S(2)}) %collective-permute-start.5) | collective-permute-done | bytes 1179680 | tf_op jit(solution)/shard_map/ppermute | solution.py:19
  45.8 1.7 slice_select_fusion
  49.7 1.4 fusion.114
  51.1 2.2 fusion.5.refs_2_
  54.3 1.4 pad_maximum_fusion.refs_12_
  55.7 8.1 %collective-permute-done.8 = bf16[256,1152]{1,0:T(8,128)(2,1)S(1)} collective-permute-done((bf16[256,1152]{1,0:T(8,128)(2,1)S(1)}, bf16[256,1152]{1,0:T(8,128)(2,1)S(1)}, u32[]{:S(2)}, u32[]{:S(2)}) %collective-permute-start.8) | collective-permute-done | bytes 589856 | tf_op jit(solution)/shard_map/ppermute | solution.py:24
  63.8 11.0 %collective-permute-done.6 = bf16[256,1152]{1,0:T(8,128)(2,1)S(1)} collective-permute-done((bf16[256,1152]{1,0:T(8,128)(2,1)S(1)}, bf16[256,1152]{1,0:T(8,128)(2,1)S(1)}, u32[]{:S(2)}, u32[]{:S(2)}) %collective-permute-start.6) | collective-permute-done | bytes 589856 | tf_op jit(solution)/shard_map/ppermute | solution.py:24
  78.6 1.7 collective-permute-start.7
  82.6 11.8 %shard_map.127 = (f32[2,512,1152]{2,1,0:T(8,128)}, f32[2,512,1]{2,1,0:T(8,128)}, bf16[2,512,1152]{2,1,0:T(8,128)(2,1)}, f32[2,512,1152]{2,1,0:T(8,128)}) custom-call(f32[1]{0:T(128)S(6)} %copy.35.mult_ref, f32[1]{0:T(128)S(6)} %copy.36.offset_ref, s32[4]{0:T(128)} %add_multiply_fusion.tops, bf16[576,1152]{1,0:T(8,128)(2,1)} %fusion.4.refs_0_, ...), custom_call_target="tpu_custom_call" | custom-call | flops 4529848320 | bytes 19468312 | tf_op jit(solution)/shard_map/pallas_call | solution.py:257
  94.4 21.9 %shard_map.128.refs_9_ = f32[2,512,1152]{2,1,0:T(8,128)} custom-call(f32[1]{0:T(128)S(6)} %copy.35.mult_ref, f32[1]{0:T(128)S(6)} %copy.36.offset_ref, s32[4]{0:T(128)} %add_multiply_fusion.tops, bf16[576,1152]{1,0:T(8,128)(2,1)} %fusion.4.refs_0_, bf16[576,1152]{1,0:T(8,128)(2,1)} %collective-permute-done.refs_1_, bf16[576,1152]{1,0:T(8,128)(2,1)} %copy-done.10, ...), custom_call_target="tpu_custom_call" | custom-call | flops 10267656192 | bytes 21823512 | tf_op jit(solution)/shard_map/pallas_call | solution.py:257
  117.8 18.4 %shard_map.129 = (bf16[2,512,1152]{2,1,0:T(8,128)(2,1)}, bf16[16,96,896]{2,1,0:T(8,128)(2,1)}) custom-call(f32[1]{0:T(128)S(6)} %copy.35.mult_ref, f32[1]{0:T(128)S(6)} %copy.36.offset_ref, s32[4]{0:T(128)} %add_multiply_fusion.tops, bf16[576,1152]{1,0:T(8,128)(2,1)} %fusion.4.refs_0_, bf16[576,1152]{1,0:T(8,128)(2,1)} %collective-permute-done.refs_1_, ...), custom_call_target="tpu_custom_call" | custom-call | flops 6492782592 | bytes 25759768 | tf_op jit(solution)/shard_map/pallas_call | solution.py:257
  136.3 6.8 %shard_map.130 = bf16[16,96,896]{2,1,0:T(8,128)(2,1)} custom-call(bf16[2,512,1152]{2,1,0:T(8,128)(2,1)} %get-tuple-element.24.in_tan, bf16[2,512,288]{2,1,0:T(8,128)(2,1)} %get-tuple-element.49.in_i, bf16[2,512,288]{2,1,0:T(8,128)(2,1)} %get-tuple-element.36.in_t), custom_call_target="tpu_custom_call" | custom-call | flops 1358954496 | bytes 6291456 | tf_op jit(solution)/shard_map/pallas_call | solution.py:257
  143.1 2.5 %add_convert_fusion = bf16[16,96,896]{2,1,0:T(8,128)(2,1)S(1)} fusion(bf16[16,96,896]{2,1,0:T(8,128)(2,1)S(1)} %collective-permute-done.12, bf16[16,96,896]{2,1,0:T(8,128)(2,1)} %shard_map.130), kind=kLoop, calls=%fused_computation | loop fusion | flops 5505024 | bytes 8257536 | tf_op jit(solution)/shard_map/convert_element_type | solution.py:358
  145.6 39.7 %all_to_all.20 = bf16[16,96,896]{2,1,0:T(8,128)(2,1)S(1)} all-to-all(bf16[16,96,896]{2,1,0:T(8,128)(2,1)S(1)} %add_convert_fusion), channel_id=1, replica_groups=mesh['y'=4,'z'=8,'xl'=2,'xh'=2,'c'=2] {'y','xl','xh'}, dimensions={0} | all-to-all | bytes 5505024 | tf_op jit(solution)/shard_map/all_to_all | solution.py:359
  185.8 14.7 %all_to_all.21 = bf16[8,12,896]{2,1,0:T(8,128)(2,1)S(1)} all-to-all(bf16[8,12,896]{2,1,0:T(8,128)(2,1)S(1)} %reshape.185), channel_id=1, replica_groups=mesh['y'=4,'z'=8,'xl'=2,'xh'=2,'c'=2] {'z'}, dimensions={0} | all-to-all | bytes 344064 | tf_op jit(solution)/shard_map/all_to_all | solution.py:361
  201.6 12.5 %all_to_all.22 = bf16[8,12,896]{2,1,0:T(8,128)(2,1)S(1)} all-to-all(bf16[8,12,896]{2,1,0:T(8,128)(2,1)S(1)} %broadcast_in_dim.9), channel_id=1, replica_groups=mesh['y'=4,'z'=8,'xl'=2,'xh'=2,'c'=2] {'z'}, dimensions={0} | all-to-all | bytes 344064 | tf_op jit(solution)/shard_map/all_to_all | solution.py:372
  215.4 3.6 %all-to-all-start.3 = ((bf16[8,96,896]{2,1,0:T(8,128)(2,1)}), bf16[8,96,896]{2,1,0:T(8,128)(2,1)S(1)}, u32[]{:S(2)}, u32[]{:S(2)}) async-start(bf16[8,96,896]{2,1,0:T(8,128)(2,1)} %broadcast_in_dim.21), calls=%async_computation.3 | async-start | bytes 2752512 | tf_op jit(solution)/shard_map/all_to_all | solution.py:374
  219.2 4.4 %fusion.7 = bf16[512,1152]{1,0:T(8,128)(2,1)} fusion(s32[1152]{0:T(1024)S(1)} %fusion.60, bf16[2,512,1152]{2,1,0:T(8,128)(2,1)} %get-tuple-element.24.in_tan), kind=kOutput, calls=%fused_computation.9 | convolution fusion | flops 1360871424 | bytes 2363904 | tf_op jit(solution)/shard_map/dot_general | solution.py:72
  223.6 3.0 %fusion.6 = bf16[512,1152]{1,0:T(8,128)(2,1)} fusion(s32[1152]{0:T(1024)S(1)} %fusion.60, bf16[2,512,1152]{2,1,0:T(8,128)(2,1)S(1)} %copy-done.2), kind=kOutput, calls=%fused_computation.8 | convolution fusion | flops 1360871424 | bytes 2367488 | tf_op jit(solution)/shard_map/dot_general | solution.py:72
  226.7 8.7 %all-to-all-done.3.parts = bf16[8,96,896]{2,1,0:T(8,128)(2,1)S(1)} async-done(((bf16[8,96,896]{2,1,0:T(8,128)(2,1)}), bf16[8,96,896]{2,1,0:T(8,128)(2,1)S(1)}, u32[]{:S(2)}, u32[]{:S(2)}) %all-to-all-start.3) | async-done | bytes 1376288 | tf_op jit(solution)/shard_map/all_to_all | solution.py:374
  235.4 4.1 %shard_map.131 = bf16[288,2304]{1,0:T(8,128)(2,1)} custom-call(bf16[8,96,896]{2,1,0:T(8,128)(2,1)S(1)} %all-to-all-done.3.parts, bf16[576,576]{1,0:T(8,128)(2,1)S(1)} %fusion.12.order), custom_call_target="tpu_custom_call" | custom-call | flops 764411904 | bytes 3366912 | tf_op jit(solution)/shard_map/pallas_call | solution.py:257
  (75 shorter events, 18.2 us)
Async XLA Ops:
  0.6 49.0 %collective-permute-start.1 = (bf16[288,2304]{1,0:T(8,128)(2,1)}, bf16[288,2304]{1,0:T(8,128)(2,1)}, u32[]{:S(2)}, u32[]{:S(2)}) collective-permute-start(bf16[288,2304]{1,0:T(8,128)(2,1)} %param.10), channel_id=1, source_target_pairs={{0,6},{2,4},{4,2},{6,0},{1,7},{3,5},{5,3},{7,1},{8,14},{10,12},{12... | collective-permute-start | bytes 3981320 | tf_op jit(solution)/shard_map/ppermute | solution.py:24
  2.7 11.6 %copy-start = (bf16[512,1152]{1,0:T(8,128)(2,1)S(1)}, bf16[512,1152]{1,0:T(8,128)(2,1)}, u32[]{:S(2)}) copy-start(bf16[512,1152]{1,0:T(8,128)(2,1)} %refs_5_.1) | copy-start | bytes 3538948
  6.0 74.3 %collective-permute-start = (bf16[576,1152]{1,0:T(8,128)(2,1)}, bf16[576,1152]{1,0:T(8,128)(2,1)}, u32[]{:S(2)}, u32[]{:S(2)}) collective-permute-start(bf16[576,1152]{1,0:T(8,128)(2,1)} %fusion.4.refs_0_), channel_id=1, source_target_pairs={{0,1},{1,0},{2,3},{3,2},{4,5},{5,4},{6,7},{7,6},{8,9},{9,8},{10,11... | collective-permute-start | bytes 3981320 | tf_op jit(solution)/shard_map/ppermute | solution.py:24
  6.0 34.5 %collective-permute-start.4 = (bf16[512,1152]{1,0:T(8,128)(2,1)}, bf16[512,1152]{1,0:T(8,128)(2,1)}, u32[]{:S(2)}, u32[]{:S(2)}) collective-permute-start(bf16[512,1152]{1,0:T(8,128)(2,1)} %refs_4_.1), channel_id=1, source_target_pairs={{0,248},{8,0},{16,8},{24,16},{32,24},{40,32},{48,40},{56,48},{64,5... | collective-permute-start | bytes 3538952 | tf_op jit(solution)/shard_map/ppermute | solution.py:19
  14.3 31.5 %collective-permute-start.5 = (bf16[512,1152]{1,0:T(8,128)(2,1)S(1)}, bf16[512,1152]{1,0:T(8,128)(2,1)}, u32[]{:S(2)}, u32[]{:S(2)}) collective-permute-start(bf16[512,1152]{1,0:T(8,128)(2,1)S(1)} %copy-done), channel_id=1, source_target_pairs={{0,8},{8,16},{16,24},{24,32},{32,40},{40,48},{48,56},{56,64},{64,7... | collective-permute-start | bytes 3538952 | tf_op jit(solution)/shard_map/ppermute | solution.py:19
  15.4 40.3 %collective-permute-start.3 = (bf16[512,1152]{1,0:T(8,128)(2,1)}, bf16[512,1152]{1,0:T(8,128)(2,1)}, u32[]{:S(2)}, u32[]{:S(2)}) collective-permute-start(bf16[512,1152]{1,0:T(8,128)(2,1)} %broadcast_select_fusion), channel_id=1, source_target_pairs={{0,4},{4,0},{1,5},{5,1},{2,6},{6,2},{3,7},{7,3},{8,12},{12,8},{9,1... | collective-permute-start | bytes 3538952 | tf_op jit(solution)/shard_map/ppermute | solution.py:24
  27.2 4.6 %copy-start.1 = (bf16[512,2,1,288]{3,0,1,2:T(8,128)(2,1)S(1)}, bf16[512,2,1,288]{3,0,1,2:T(8,128)(2,1)}, u32[]{:S(2)}) copy-start(bf16[512,2,1,288]{3,0,1,2:T(8,128)(2,1)} %copy.30) | copy-start | bytes 1769476
  47.5 16.3 %collective-permute-start.8 = (bf16[256,1152]{1,0:T(8,128)(2,1)S(1)}, bf16[256,1152]{1,0:T(8,128)(2,1)S(1)}, u32[]{:S(2)}, u32[]{:S(2)}) collective-permute-start(bf16[256,1152]{1,0:T(8,128)(2,1)S(1)} %get-tuple-element.30), channel_id=1, source_target_pairs={{0,4},{4,0},{1,5},{5,1},{2,6},{6,2},{3,7},{7,3},{8,12},{12,8},{9,1... | collective-permute-start | bytes 1769480 | tf_op jit(solution)/shard_map/ppermute | solution.py:24
  48.8 26.1 %collective-permute-start.6 = (bf16[256,1152]{1,0:T(8,128)(2,1)S(1)}, bf16[256,1152]{1,0:T(8,128)(2,1)S(1)}, u32[]{:S(2)}, u32[]{:S(2)}) collective-permute-start(bf16[256,1152]{1,0:T(8,128)(2,1)S(1)} %get-tuple-element.31), channel_id=1, source_target_pairs={{0,4},{4,0},{1,5},{5,1},{2,6},{6,2},{3,7},{7,3},{8,12},{12,8},{9,1... | collective-permute-start | bytes 1769480 | tf_op jit(solution)/shard_map/ppermute | solution.py:24
  53.3 2.4 %copy-start.10 = (bf16[576,1152]{1,0:T(8,128)(2,1)}, bf16[576,1152]{1,0:T(8,128)(2,1)S(1)}, u32[]{:S(2)}) copy-start(bf16[576,1152]{1,0:T(8,128)(2,1)S(1)} %fusion.5.refs_2_) | copy-start | bytes 3981316
  53.3 28.2 %collective-permute-start.2 = (bf16[576,1152]{1,0:T(8,128)(2,1)S(1)}, bf16[576,1152]{1,0:T(8,128)(2,1)S(1)}, u32[]{:S(2)}, u32[]{:S(2)}) collective-permute-start(bf16[576,1152]{1,0:T(8,128)(2,1)S(1)} %fusion.5.refs_2_), channel_id=1, source_target_pairs={{0,1},{1,0},{2,3},{3,2},{4,5},{5,4},{6,7},{7,6},{8,9},{9,8},{10,11... | collective-permute-start | bytes 3981320 | tf_op jit(solution)/shard_map/ppermute | solution.py:24
  76.1 18.3 %copy-start.3 = (bf16[256,1152]{1,0:T(8,128)(2,1)}, bf16[256,1152]{1,0:T(8,128)(2,1)S(1)}, u32[]{:S(2)}) copy-start(bf16[256,1152]{1,0:T(8,128)(2,1)S(1)} %get-tuple-element.35.refs_6_) | copy-start | bytes 1769476
  76.1 18.3 %copy-start.5 = (bf16[256,1152]{1,0:T(8,128)(2,1)}, bf16[256,1152]{1,0:T(8,128)(2,1)S(1)}, u32[]{:S(2)}) copy-start(bf16[256,1152]{1,0:T(8,128)(2,1)S(1)} %get-tuple-element.34.refs_8_) | copy-start | bytes 1769476
  76.1 40.2 %collective-permute-start.10 = (bf16[256,1152]{1,0:T(8,128)(2,1)S(1)}, bf16[256,1152]{1,0:T(8,128)(2,1)S(1)}, u32[]{:S(2)}, u32[]{:S(2)}) collective-permute-start(bf16[256,1152]{1,0:T(8,128)(2,1)S(1)} %get-tuple-element.34.refs_8_), channel_id=1, source_target_pairs={{0,248},{8,0},{16,8},{24,16},{32,24},{40,32},{48,40},{56,48},{64,5... | collective-permute-start | bytes 1769480 | tf_op jit(solution)/shard_map/ppermute | solution.py:19
  78.1 16.2 %copy-start.4 = (bf16[256,1152]{1,0:T(8,128)(2,1)}, bf16[256,1152]{1,0:T(8,128)(2,1)S(1)}, u32[]{:S(2)}) copy-start(bf16[256,1152]{1,0:T(8,128)(2,1)S(1)} %get-tuple-element.33.refs_7_) | copy-start | bytes 1769476
  78.2 16.2 %copy-start.6 = (bf16[256,1152]{1,0:T(8,128)(2,1)}, bf16[256,1152]{1,0:T(8,128)(2,1)S(1)}, u32[]{:S(2)}) copy-start(bf16[256,1152]{1,0:T(8,128)(2,1)S(1)} %get-tuple-element.32.refs_9_) | copy-start | bytes 1769476
  78.2 38.2 %collective-permute-start.11 = (bf16[256,1152]{1,0:T(8,128)(2,1)S(1)}, bf16[256,1152]{1,0:T(8,128)(2,1)S(1)}, u32[]{:S(2)}, u32[]{:S(2)}) collective-permute-start(bf16[256,1152]{1,0:T(8,128)(2,1)S(1)} %get-tuple-element.32.refs_9_), channel_id=1, source_target_pairs={{0,248},{8,0},{16,8},{24,16},{32,24},{40,32},{48,40},{56,48},{64,5... | collective-permute-start | bytes 1769480 | tf_op jit(solution)/shard_map/ppermute | solution.py:19
  78.6 37.8 %collective-permute-start.7 = (bf16[256,1152]{1,0:T(8,128)(2,1)S(1)}, bf16[256,1152]{1,0:T(8,128)(2,1)S(1)}, u32[]{:S(2)}, u32[]{:S(2)}) collective-permute-start(bf16[256,1152]{1,0:T(8,128)(2,1)S(1)} %get-tuple-element.35.refs_6_), channel_id=1, source_target_pairs={{0,8},{8,16},{16,24},{24,32},{32,40},{40,48},{48,56},{56,64},{64,7... | collective-permute-start | bytes 1769480 | tf_op jit(solution)/shard_map/ppermute | solution.py:19
  80.3 36.1 %collective-permute-start.9 = (bf16[256,1152]{1,0:T(8,128)(2,1)S(1)}, bf16[256,1152]{1,0:T(8,128)(2,1)S(1)}, u32[]{:S(2)}, u32[]{:S(2)}) collective-permute-start(bf16[256,1152]{1,0:T(8,128)(2,1)S(1)} %get-tuple-element.33.refs_7_), channel_id=1, source_target_pairs={{0,8},{8,16},{16,24},{24,32},{32,40},{40,48},{48,56},{56,64},{64,7... | collective-permute-start | bytes 1769480 | tf_op jit(solution)/shard_map/ppermute | solution.py:19
  81.5 1.1 copy-start.11
  116.3 0.8 copy-start.12
  116.3 1.0 copy-start.13
  116.4 1.2 copy-start.14
  116.4 1.4 copy-start.15
  136.2 6.9 %collective-permute-start.12 = (bf16[16,96,896]{2,1,0:T(8,128)(2,1)}, bf16[16,96,896]{2,1,0:T(8,128)(2,1)S(1)}, u32[]{:S(2)}, u32[]{:S(2)}) collective-permute-start(bf16[16,96,896]{2,1,0:T(8,128)(2,1)} %get-tuple-element.25), channel_id=1, source_target_pairs={{0,1},{1,0},{2,3},{3,2},{4,5},{5,4},{6,7},{7,6},{8,9},{9,8},{10,11... | collective-permute-start | bytes 8257544 | tf_op jit(solution)/shard_map/ppermute | solution.py:24
  185.7 15.0 %copy-start.7 = (f32[288,36]{0,1:T(8,128)S(1)}, f32[288,36]{0,1:T(8,128)}, u32[]{:S(2)}) copy-start(f32[288,36]{0,1:T(8,128)} %param.13) | copy-start | bytes 124420
  185.7 15.0 %copy-start.8 = (f32[288,36]{0,1:T(8,128)S(1)}, f32[288,36]{0,1:T(8,128)}, u32[]{:S(2)}) copy-start(f32[288,36]{0,1:T(8,128)} %param.15) | copy-start | bytes 124420
  185.7 15.0 %copy-start.9 = (f32[288,36]{0,1:T(8,128)S(1)}, f32[288,36]{0,1:T(8,128)}, u32[]{:S(2)}) copy-start(f32[288,36]{0,1:T(8,128)} %param.14) | copy-start | bytes 124420
  215.4 20.0 %all-to-all-start.3 = ((bf16[8,96,896]{2,1,0:T(8,128)(2,1)}), bf16[8,96,896]{2,1,0:T(8,128)(2,1)S(1)}, u32[]{:S(2)}, u32[]{:S(2)}) async-start(bf16[8,96,896]{2,1,0:T(8,128)(2,1)} %broadcast_in_dim.21), calls=%async_computation.3 | async-start | bytes 2752512 | tf_op jit(solution)/shard_map/all_to_all | solution.py:374
  219.2 4.5 %copy-start.2 = (bf16[2,512,1152]{2,1,0:T(8,128)(2,1)S(1)}, bf16[2,512,1152]{2,1,0:T(8,128)(2,1)}, u32[]{:S(2)}) copy-start(bf16[2,512,1152]{2,1,0:T(8,128)(2,1)} %get-tuple-element.24.in_tan) | copy-start | bytes 7077892

commit v2 on v1

--- a/solution.py
+++ b/solution.py
@@ -1,5 +1,3 @@
-import functools
-
 import jax
 import jax.numpy as jnp
 from jax import lax
@@ -82,11 +80,26 @@
     def __init__(self, sems):
         self.sems, self.used = sems, 0
 
-    def start(self, source, target):
-        copy = pltpu.make_async_copy(source, target, self.sems.at[self.used])
+    def plan(self, source, target):
         self.used += 1
-        copy.start()
-        return copy
+        return pltpu.make_async_copy(source, target, self.sems.at[self.used - 1])
+
+
+def start(*groups):
+    for group in groups:
+        for copy in group:
+            copy.start()
+
+
+def arrive(turn, ready, stride=1, extra=()):
+    for n, copies in enumerate(ready):
+
+        def land(n=n, copies=copies):
+            wait(copies)
+            if n == 0:
+                start(*ready[1:], *extra)
+
+        pl.when(turn == n * stride)(land)
 
 
 def load_weights(loads, tops, shards, w, side):
@@ -94,13 +107,13 @@
     for n, shard in enumerate(shards):
         top = pl.multiple_of(tops[n], 32)
         source = shard.at[pl.ds(side * SHARE, SHARE), :]
-        copies.append(loads.start(source, w.at[side, pl.ds(top, SHARE), :]))
+        copies.append(loads.plan(source, w.at[side, pl.ds(top, SHARE), :]))
     return copies
 
 
 def load_rows(loads, pieces, raw):
     rows = pieces[0].shape[0]
-    return [loads.start(p, raw.at[pl.ds(n * rows, rows), :]) for n, p in enumerate(pieces)]
+    return [loads.plan(p, raw.at[pl.ds(n * rows, rows), :]) for n, p in enumerate(pieces)]
 
 
 def wait(*groups):
@@ -126,9 +139,10 @@
             load_weights(loads, tops, shards, w, side) + load_rows(loads, [rows], raw.at[side])
         )
 
+    start(ready[0])
+
     def step(side, carry):
-        for n in range(2):
-            pl.when(side == n)(functools.partial(wait, ready[n]))
+        arrive(side, ready)
         u, inv = project(raw[side], w[side])
         unit[side] = u
         norm[side] = inv
@@ -156,15 +170,16 @@
         ready.append(
             load_weights(loads, tops, shards, w, 1 - side)
             + load_rows(loads, [two], raw.at[side])
-            + [loads.start(in_low.at[side], low.at[side])]
-            + [loads.start(in_acc.at[side], acc.at[side])]
+            + [loads.plan(in_low.at[side], low.at[side])]
+            + [loads.plan(in_acc.at[side], acc.at[side])]
         )
     for side, ones in enumerate((texts, images)):
         ready.append(load_rows(loads, ones, raw.at[2 + side]))
 
+    start(ready[0])
+
     def step(turn, carry):
-        for n in range(4):
-            pl.when(turn == n)(functools.partial(wait, ready[n]))
+        arrive(turn, ready)
         side = lax.rem(turn, 2)
         acc[side] += meet(raw[turn], w[1 - side], low.at[side], mult, offset)
         return carry
@@ -175,7 +190,8 @@
 def tail_kernel(mult_ref, offset_ref, tops, *refs):
     shards, refs = refs[:4], refs[4:]
     texts, images, refs = refs[:PIECES], refs[PIECES : 2 * PIECES], refs[2 * PIECES :]
-    in_low, in_acc, in_unit, in_norm, in_x, tan, chunks, w, raw, low, acc, unit, norm, x, sems = refs
+    in_low, in_acc, in_unit, in_norm, *in_x = refs[:8]
+    tan, chunks, w, raw, low, acc, unit, norm, x, sems = refs[8:]
     mult, offset = mult_ref[0], offset_ref[0]
     loads = Loads(sems)
     ready = []
@@ -183,14 +199,16 @@
         ready.append(
             load_weights(loads, tops, shards, w, 1 - side)
             + load_rows(loads, rows, raw.at[side])
-            + [loads.start(in_low.at[side], low.at[side])]
-            + [loads.start(in_acc.at[side], acc.at[side])]
+            + [loads.plan(in_low.at[side], low.at[side])]
+            + [loads.plan(in_acc.at[side], acc.at[side])]
         )
-    last = [loads.start(in_unit, unit), loads.start(in_norm, norm), loads.start(in_x, x)]
+    last = [loads.plan(in_unit, unit), loads.plan(in_norm, norm)]
+    last += [loads.plan(source, x.at[n // 2, n % 2]) for n, source in enumerate(in_x)]
+
+    start(ready[0])
 
     def step(side, carry):
-        for n in range(2):
-            pl.when(side == n)(functools.partial(wait, ready[n]))
+        arrive(side, ready, extra=(last,))
         acc[side] += meet(raw[side], w[1 - side], low.at[side], mult, offset)
         return carry
 
@@ -211,8 +229,7 @@
 
 def fill(chunks, tan, x, ready=()):
     def step(turn, carry):
-        for n, copies in enumerate(ready):
-            pl.when(turn == 2 * n)(functools.partial(wait, copies))
+        arrive(turn, ready, stride=2)
         t, xh = turn // 2, lax.rem(turn, 2)
         g = dot(tan[t], x[t, xh], ((0,), (0,)))
         for block in range(4):
@@ -226,11 +243,14 @@
     lax.fori_loop(0, 4, step, 0)
 
 
-def keep_kernel(in_tan, in_i, in_t, chunks, tan, x, sems):
+def keep_kernel(in_tan, *refs):
+    in_x, (chunks, tan, x, sems) = refs[:4], refs[4:]
     loads = Loads(sems)
     ready = []
-    for side, source in enumerate((in_i, in_t)):
-        ready.append([loads.start(source, x.at[side]), loads.start(in_tan.at[side], tan.at[side])])
+    for t in range(2):
+        ready.append([loads.plan(in_tan.at[t], tan.at[t])])
+        ready[t] += [loads.plan(in_x[2 * t + xh], x.at[t, xh]) for xh in range(2)]
+    start(ready[0])
     fill(chunks, tan, x, ready)
 
 
@@ -301,11 +321,11 @@
     c = lax.axis_index("c")
 
     def columns(rows, core):
-        parts = rows.reshape(ROWS, 2, 2, SHARE)
-        return jnp.where(core == 0, parts[:, :, 0], parts[:, :, 1]).transpose(1, 0, 2)
-
-    give_x = jnp.stack([columns(img, 1 - c), columns(txt, 1 - c)])
-    keep_i, keep_t = columns(img, c), columns(txt, c)
+        cuts = [rows[:, n * SHARE : (n + 1) * SHARE] for n in range(4)]
+        return [jnp.where(core == 0, cuts[2 * xh], cuts[2 * xh + 1]) for xh in range(2)]
+
+    give_x = columns(img, 1 - c) + columns(txt, 1 - c)
+    keep_x = columns(img, c) + columns(txt, c)
 
     def both(shape, dtype):
         return shaped((2, *shape), dtype), pltpu.VMEM((2, *shape), dtype)
@@ -337,7 +357,7 @@
     tan, give = call(
         tail_kernel,
         (low, chunk),
-        (*scalars, *shards, *three_t, *three_i, low_of, acc, unit_of, norm_of, give_x),
+        (*scalars, *shards, *three_t, *three_i, low_of, acc, unit_of, norm_of, *give_x),
         mac * (3 * WIDTH + 4 * ROWS),
         scalars=3,
         scratch=(vw, vlow, vlow, vbig, vbig, vflat, pltpu.VMEM((2, 2, ROWS, SHARE), bf16)),
@@ -347,7 +367,7 @@
     (keep,) = call(
         keep_kernel,
         (chunk,),
-        (tan, keep_i, keep_t),
+        (tan, *keep_x),
         mac * WIDTH,
         scratch=(vlow, pltpu.VMEM((2, 2, ROWS, SHARE), bf16)),
         anywhere=True,

time: 240 us -> 239 us (level)
  local copies, waits for them, and re-layouts: 19.5 us -> 5.74 us
  waiting for transfers between devices: 39 us -> 47.8 us
    ppermute x6, waiting for transfers between devices: 11.1 us -> 23.8 us  [shifted(): lax.ppermute(value, LINE, [(i, (i + steps) % count) for i in range(count)])]
    unnamed x38 -> x28, local copies, waits for them, and re-layouts: 12.9 us -> 1.39 us
    ppermute x7, waiting for transfers between devices: 19.2 us -> 15.4 us  [swapped(): return lax.ppermute(value, axes, [(i, count - 1 - i) for i in range(count)])]
    ppermute x6, starting transfers between devices: 12.5 us -> 15.8 us  [shifted(): lax.ppermute(value, LINE, [(i, (i + steps) % count) for i in range(count)])]
    transpose x1 -> x0, other arithmetic: 2.88 us -> none  [columns(): jnp.where(core == 0, parts[:, :, 0], parts[:, :, 1]).transpose(1, 0, 2)]
    select_n x0 -> x1, other arithmetic: none -> 2.64 us  [columns(): jnp.where(core == 0, cuts[2 * xh], cuts[2 * xh + 1])]
  transfers between devices with their start and end apart: 14 -> 14, of which waited for: 5 -> 5; matrix products, arithmetic and copies ran while one was open for 16% -> 11% of each run, Pallas kernels for 17% -> 17%
where the time goes in v2:
time: 239 us; the launch traced here: 238 us
  blocking collectives  68.2 us (29%)
  Pallas kernels  63 us (26%)
  waiting for transfers between devices  47.8 us (20%)
  starting transfers between devices  23.5 us (10%)
  matrix products  14.1 us (6%)
  other arithmetic  13.3 us (6%)
  local copies, waits for them, and re-layouts  5.74 us (2%)
    pallas_call x5, Pallas kernels, call(): pl.pallas_call(kernel, out_shape=outs, in_specs=[SMEM] * scalars + [spec]...  63 us
    all_to_all x1, blocking collectives, inner(): parts = lax.all_to_all(chip, ('y', 'xl', 'xh'), 0, 0, tiled=True)  39.5 us
    ppermute x6, waiting for transfers between devices, shifted(): lax.ppermute(value, LINE, [(i, (i + steps) % count) for i in range(count)])  23.8 us
    all_to_all x1, blocking collectives, inner(): parts = lax.all_to_all(plane.reshape(8, 12, LANES), 'z', 0, 0, tiled=True)  16.2 us
    ppermute x6, starting transfers between devices, shifted(): lax.ppermute(value, LINE, [(i, (i + steps) % count) for i in range(count)])  15.8 us
    ppermute x7, waiting for transfers between devices, swapped(): return lax.ppermute(value, axes, [(i, count - 1 - i) for i in range(count)])  15.4 us
    dot_general x4, matrix products, dot(): lax.dot_general(left, right, (dims, ((), ())), preferred_element_type=jnp...  14.1 us
    all_to_all x1, blocking collectives, inner(): lax.all_to_all(jnp.broadcast_to(mine, (8, 12, LANES)), 'z', 0, 0, tiled=T...  12.5 us
  transfers between devices with their start and end apart: 14, of which 5 were waited for; matrix products, arithmetic and copies ran while one was open for 11% of the time, Pallas kernels for 17%

profile of v2, /device:TPU:4, one launch (start us, length us, event | category | flops | bytes accessed | tf_op | source)
XLA Modules:
  0.0 237.9 jit_solution(16982879564958504607)
XLA Ops:
  1.3 8.3 %collective-permute-start.4 = (bf16[512,1152]{1,0:T(8,128)(2,1)}, bf16[512,1152]{1,0:T(8,128)(2,1)}, u32[]{:S(2)}, u32[]{:S(2)}) collective-permute-start(bf16[512,1152]{1,0:T(8,128)(2,1)} %refs_4_.1), channel_id=1, source_target_pairs={{0,248},{8,0},{16,8},{24,16},{32,24},{40,32},{48,40},{56,48},{64,5... | collective-permute-start | bytes 3538952 | tf_op jit(solution)/shard_map/ppermute | solution.py:17
  9.6 1.4 fusion.115
  11.0 3.3 %fusion.4.refs_0_ = bf16[576,1152]{1,0:T(8,128)(2,1)} fusion(s32[1152]{0:T(1024)S(1)} %fusion.60, bf16[288,1152]{1,0:T(8,128)(2,1)S(1)} %get-tuple-element.39, bf16[288,1152]{1,0:T(8,128)(2,1)S(1)} %get-tuple-element.38), kind=kOutput, calls=%fused_computation.6 | convolution fusion | flops 1533468672 | bytes 2658816 | tf_op jit(solution)/shard_map/dot_general | solution.py:70
  14.3 1.1 broadcast_select_fusion
  15.5 1.1 collective-permute-start.3
  16.6 18.2 %collective-permute-done.4.refs_5_ = bf16[512,1152]{1,0:T(8,128)(2,1)} collective-permute-done((bf16[512,1152]{1,0:T(8,128)(2,1)}, bf16[512,1152]{1,0:T(8,128)(2,1)}, u32[]{:S(2)}, u32[]{:S(2)}) %collective-permute-start.4) | collective-permute-done | bytes 1179680 | tf_op jit(solution)/shard_map/ppermute | solution.py:17
  34.8 5.5 %collective-permute-done.5.refs_4_ = bf16[512,1152]{1,0:T(8,128)(2,1)} collective-permute-done((bf16[512,1152]{1,0:T(8,128)(2,1)}, bf16[512,1152]{1,0:T(8,128)(2,1)}, u32[]{:S(2)}, u32[]{:S(2)}) %collective-permute-start.5) | collective-permute-done | bytes 1179680 | tf_op jit(solution)/shard_map/ppermute | solution.py:17
  40.3 2.7 %slice_select_fusion = (bf16[256,1152]{1,0:T(8,128)(2,1)}, bf16[256,1152]{1,0:T(8,128)(2,1)}) fusion(bf16[512,1152]{1,0:T(8,128)(2,1)} %collective-permute-done.5.refs_4_, bf16[512,1152]{1,0:T(8,128)(2,1)} %collective-permute-done.4.refs_5_, pred[]{:T(512)S(6)} %eq.72), kind=kLoop, calls=%fused_computation.27 | loop fusion | flops 589824 | bytes 3538945 | tf_op jit(solution)/shard_map/jit(_where)/select_n | solution.py:46
  43.1 1.1 collective-permute-start.8
  45.1 1.4 fusion.114
  46.5 3.3 %fusion.5.refs_2_ = bf16[576,1152]{1,0:T(8,128)(2,1)} fusion(s32[1152]{0:T(1024)S(1)} %fusion.60, bf16[288,1152]{1,0:T(8,128)(2,1)S(1)} %get-tuple-element.37, bf16[288,1152]{1,0:T(8,128)(2,1)S(1)} %get-tuple-element.36), kind=kOutput, calls=%fused_computation.7 | convolution fusion | flops 1533468672 | bytes 2658816 | tf_op jit(solution)/shard_map/dot_general | solution.py:70
  49.8 2.6 %broadcast_select_fusion.5 = (bf16[512,288]{1,0:T(8,128)(2,1)}, bf16[512,288]{1,0:T(8,128)(2,1)}, bf16[512,288]{1,0:T(8,128)(2,1)}, bf16[512,288]{1,0:T(8,128)(2...) fusion(pred[]{:T(512)S(6)} %eq.74, ...), kind=kLoop, calls=%fused_computation.34 | loop fusion | flops 1179648 | bytes 4718594 | tf_op jit(solution)/shard_map/jit(_where)/select_n | solution.py:325
  54.3 5.3 %collective-permute-done.8 = bf16[256,1152]{1,0:T(8,128)(2,1)} collective-permute-done((bf16[256,1152]{1,0:T(8,128)(2,1)}, bf16[256,1152]{1,0:T(8,128)(2,1)}, u32[]{:S(2)}, u32[]{:S(2)}) %collective-permute-start.8) | collective-permute-done | bytes 589856 | tf_op jit(solution)/shard_map/ppermute | solution.py:22
  59.6 10.1 %collective-permute-done.6 = bf16[256,1152]{1,0:T(8,128)(2,1)} collective-permute-done((bf16[256,1152]{1,0:T(8,128)(2,1)}, bf16[256,1152]{1,0:T(8,128)(2,1)}, u32[]{:S(2)}, u32[]{:S(2)}) %collective-permute-start.6) | collective-permute-done | bytes 589856 | tf_op jit(solution)/shard_map/ppermute | solution.py:22
  69.7 1.2 broadcast_select_fusion.2
  70.9 5.2 %collective-permute-start.10 = (bf16[256,1152]{1,0:T(8,128)(2,1)S(1)}, bf16[256,1152]{1,0:T(8,128)(2,1)S(1)}, u32[]{:S(2)}, u32[]{:S(2)}) collective-permute-start(bf16[256,1152]{1,0:T(8,128)(2,1)S(1)} %get-tuple-element.34.refs_8_), channel_id=1, source_target_pairs={{0,248},{8,0},{16,8},{24,16},{32,24},{40,32},{48,40},{56,48},{64,5... | collective-permute-start | bytes 1769480 | tf_op jit(solution)/shard_map/ppermute | solution.py:17
  76.1 1.2 broadcast_select_fusion.1
  77.8 1.7 collective-permute-start.7
  79.6 11.8 %shard_map.127 = (f32[2,512,1152]{2,1,0:T(8,128)}, f32[2,512,1]{2,1,0:T(8,128)}, bf16[2,512,1152]{2,1,0:T(8,128)(2,1)}, f32[2,512,1152]{2,1,0:T(8,128)}) custom-call(f32[1]{0:T(128)S(6)} %copy.19.mult_ref, f32[1]{0:T(128)S(6)} %copy.20.offset_ref, s32[4]{0:T(128)} %add_multiply_fusion.tops, bf16[576,1152]{1,0:T(8,128)(2,1)} %fusion.4.refs_0_, ...), custom_call_target="tpu_custom_call" | custom-call | flops 4529848320 | bytes 19468312 | tf_op jit(solution)/shard_map/pallas_call | solution.py:277
  91.4 21.9 %shard_map.128.refs_9_ = f32[2,512,1152]{2,1,0:T(8,128)} custom-call(f32[1]{0:T(128)S(6)} %copy.19.mult_ref, f32[1]{0:T(128)S(6)} %copy.20.offset_ref, s32[4]{0:T(128)} %add_multiply_fusion.tops, bf16[576,1152]{1,0:T(8,128)(2,1)} %fusion.4.refs_0_, bf16[576,1152]{1,0:T(8,128)(2,1)} %collective-permute-done.refs_1_, bf16[576,1152]{1,0:T(8,128)(2,1)} %fusion.5.refs_2_, ...), custom_call_target="tpu_custom_call" | custom-call | flops 10267656192 | bytes 21823512 | tf_op jit(solution)/shard_map/pallas_call | solution.py:277
  114.7 18.5 %shard_map.129 = (bf16[2,512,1152]{2,1,0:T(8,128)(2,1)}, bf16[16,96,896]{2,1,0:T(8,128)(2,1)}) custom-call(f32[1]{0:T(128)S(6)} %copy.19.mult_ref, f32[1]{0:T(128)S(6)} %copy.20.offset_ref, s32[4]{0:T(128)} %add_multiply_fusion.tops, bf16[576,1152]{1,0:T(8,128)(2,1)} %fusion.4.refs_0_, bf16[576,1152]{1,0:T(8,128)(2,1)} %collective-permute-done.refs_1_, ...), custom_call_target="tpu_custom_call" | custom-call | flops 6492782592 | bytes 25759768 | tf_op jit(solution)/shard_map/pallas_call | solution.py:277
  133.5 6.8 %shard_map.130 = bf16[16,96,896]{2,1,0:T(8,128)(2,1)} custom-call(bf16[2,512,1152]{2,1,0:T(8,128)(2,1)} %get-tuple-element.24.in_tan, bf16[512,288]{1,0:T(8,128)(2,1)} %get-tuple-element.48.refs_0_, bf16[512,288]{1,0:T(8,128)(2,1)} %get-tuple-element.51.refs_1_, bf16[512,288]{1,0:T(8,128)(2,1)} %get-tuple-element.43.refs_2_, ...), custom_call_target="tpu_custom_call" | custom-call | flops 1358954496 | bytes 6291456 | tf_op jit(solution)/shard_map/pallas_call | solution.py:277
  140.3 2.5 %add_convert_fusion = bf16[16,96,896]{2,1,0:T(8,128)(2,1)S(1)} fusion(bf16[16,96,896]{2,1,0:T(8,128)(2,1)S(1)} %collective-permute-done.12, bf16[16,96,896]{2,1,0:T(8,128)(2,1)} %shard_map.130), kind=kLoop, calls=%fused_computation | loop fusion | flops 5505024 | bytes 8257536 | tf_op jit(solution)/shard_map/convert_element_type | solution.py:378
  142.8 39.5 %all_to_all.20 = bf16[16,96,896]{2,1,0:T(8,128)(2,1)S(1)} all-to-all(bf16[16,96,896]{2,1,0:T(8,128)(2,1)S(1)} %add_convert_fusion), channel_id=1, replica_groups=mesh['y'=4,'z'=8,'xl'=2,'xh'=2,'c'=2] {'y','xl','xh'}, dimensions={0} | all-to-all | bytes 5505024 | tf_op jit(solution)/shard_map/all_to_all | solution.py:379
  182.8 16.2 %all_to_all.21 = bf16[8,12,896]{2,1,0:T(8,128)(2,1)S(1)} all-to-all(bf16[8,12,896]{2,1,0:T(8,128)(2,1)S(1)} %reshape.167), channel_id=1, replica_groups=mesh['y'=4,'z'=8,'xl'=2,'xh'=2,'c'=2] {'z'}, dimensions={0} | all-to-all | bytes 344064 | tf_op jit(solution)/shard_map/all_to_all | solution.py:381
  200.1 12.5 %all_to_all.22 = bf16[8,12,896]{2,1,0:T(8,128)(2,1)S(1)} all-to-all(bf16[8,12,896]{2,1,0:T(8,128)(2,1)S(1)} %broadcast_in_dim.9), channel_id=1, replica_groups=mesh['y'=4,'z'=8,'xl'=2,'xh'=2,'c'=2] {'z'}, dimensions={0} | all-to-all | bytes 344064 | tf_op jit(solution)/shard_map/all_to_all | solution.py:392
  212.7 1.2 broadcast_in_dim.21
  213.9 3.6 %all-to-all-start.3 = ((bf16[8,96,896]{2,1,0:T(8,128)(2,1)}), bf16[8,96,896]{2,1,0:T(8,128)(2,1)S(1)}, u32[]{:S(2)}, u32[]{:S(2)}) async-start(bf16[8,96,896]{2,1,0:T(8,128)(2,1)} %broadcast_in_dim.21), calls=%async_computation.3 | async-start | bytes 2752512 | tf_op jit(solution)/shard_map/all_to_all | solution.py:394
  217.7 4.4 %fusion.7 = bf16[512,1152]{1,0:T(8,128)(2,1)} fusion(s32[1152]{0:T(1024)S(1)} %fusion.60, bf16[2,512,1152]{2,1,0:T(8,128)(2,1)} %get-tuple-element.24.in_tan), kind=kOutput, calls=%fused_computation.9 | convolution fusion | flops 1360871424 | bytes 2363904 | tf_op jit(solution)/shard_map/dot_general | solution.py:70
  222.1 3.0 %fusion.6 = bf16[512,1152]{1,0:T(8,128)(2,1)} fusion(s32[1152]{0:T(1024)S(1)} %fusion.60, bf16[2,512,1152]{2,1,0:T(8,128)(2,1)S(1)} %copy-done.2), kind=kOutput, calls=%fused_computation.8 | convolution fusion | flops 1360871424 | bytes 2367488 | tf_op jit(solution)/shard_map/dot_general | solution.py:70
  225.2 8.7 %all-to-all-done.3.parts = bf16[8,96,896]{2,1,0:T(8,128)(2,1)S(1)} async-done(((bf16[8,96,896]{2,1,0:T(8,128)(2,1)}), bf16[8,96,896]{2,1,0:T(8,128)(2,1)S(1)}, u32[]{:S(2)}, u32[]{:S(2)}) %all-to-all-start.3) | async-done | bytes 1376288 | tf_op jit(solution)/shard_map/all_to_all | solution.py:394
  233.9 4.1 %shard_map.131 = bf16[288,2304]{1,0:T(8,128)(2,1)} custom-call(bf16[8,96,896]{2,1,0:T(8,128)(2,1)S(1)} %all-to-all-done.3.parts, bf16[576,576]{1,0:T(8,128)(2,1)S(1)} %fusion.12.order), custom_call_target="tpu_custom_call" | custom-call | flops 764411904 | bytes 3366912 | tf_op jit(solution)/shard_map/pallas_call | solution.py:277
  (62 shorter events, 6.2 us)
Async XLA Ops:
  0.6 44.5 %collective-permute-start.1 = (bf16[288,2304]{1,0:T(8,128)(2,1)}, bf16[288,2304]{1,0:T(8,128)(2,1)}, u32[]{:S(2)}, u32[]{:S(2)}) collective-permute-start(bf16[288,2304]{1,0:T(8,128)(2,1)} %param.10), channel_id=1, source_target_pairs={{0,6},{2,4},{4,2},{6,0},{1,7},{3,5},{5,3},{7,1},{8,14},{10,12},{12... | collective-permute-start | bytes 3981320 | tf_op jit(solution)/shard_map/ppermute | solution.py:22
  1.3 33.6 %collective-permute-start.4 = (bf16[512,1152]{1,0:T(8,128)(2,1)}, bf16[512,1152]{1,0:T(8,128)(2,1)}, u32[]{:S(2)}, u32[]{:S(2)}) collective-permute-start(bf16[512,1152]{1,0:T(8,128)(2,1)} %refs_4_.1), channel_id=1, source_target_pairs={{0,248},{8,0},{16,8},{24,16},{32,24},{40,32},{48,40},{56,48},{64,5... | collective-permute-start | bytes 3538952 | tf_op jit(solution)/shard_map/ppermute | solution.py:17
  9.6 30.8 %collective-permute-start.5 = (bf16[512,1152]{1,0:T(8,128)(2,1)}, bf16[512,1152]{1,0:T(8,128)(2,1)}, u32[]{:S(2)}, u32[]{:S(2)}) collective-permute-start(bf16[512,1152]{1,0:T(8,128)(2,1)} %refs_5_.1), channel_id=1, source_target_pairs={{0,8},{8,16},{16,24},{24,32},{32,40},{40,48},{48,56},{56,64},{64,7... | collective-permute-start | bytes 3538952 | tf_op jit(solution)/shard_map/ppermute | solution.py:17
  11.0 3.3 %copy-start = (bf16[512,1152]{1,0:T(8,128)(2,1)S(1)}, bf16[512,1152]{1,0:T(8,128)(2,1)}, u32[]{:S(2)}) copy-start(bf16[512,1152]{1,0:T(8,128)(2,1)} %refs_5_.1) | copy-start | bytes 3538948
  11.0 3.3 %copy-start.1 = (bf16[512,1152]{1,0:T(8,128)(2,1)S(1)}, bf16[512,1152]{1,0:T(8,128)(2,1)}, u32[]{:S(2)}) copy-start(bf16[512,1152]{1,0:T(8,128)(2,1)} %refs_4_.1) | copy-start | bytes 3538948
  14.3 65.2 %collective-permute-start = (bf16[576,1152]{1,0:T(8,128)(2,1)}, bf16[576,1152]{1,0:T(8,128)(2,1)}, u32[]{:S(2)}, u32[]{:S(2)}) collective-permute-start(bf16[576,1152]{1,0:T(8,128)(2,1)} %fusion.4.refs_0_), channel_id=1, source_target_pairs={{0,1},{1,0},{2,3},{3,2},{4,5},{5,4},{6,7},{7,6},{8,9},{9,8},{10,11... | collective-permute-start | bytes 3981320 | tf_op jit(solution)/shard_map/ppermute | solution.py:22
  15.5 38.9 %collective-permute-start.3 = (bf16[512,1152]{1,0:T(8,128)(2,1)}, bf16[512,1152]{1,0:T(8,128)(2,1)S(1)}, u32[]{:S(2)}, u32[]{:S(2)}) collective-permute-start(bf16[512,1152]{1,0:T(8,128)(2,1)} %broadcast_select_fusion), channel_id=1, source_target_pairs={{0,4},{4,0},{1,5},{5,1},{2,6},{6,2},{3,7},{7,3},{8,12},{12,8},{9,1... | collective-permute-start | bytes 3538952 | tf_op jit(solution)/shard_map/ppermute | solution.py:22
  43.1 16.5 %collective-permute-start.8 = (bf16[256,1152]{1,0:T(8,128)(2,1)}, bf16[256,1152]{1,0:T(8,128)(2,1)}, u32[]{:S(2)}, u32[]{:S(2)}) collective-permute-start(bf16[256,1152]{1,0:T(8,128)(2,1)} %get-tuple-element.30), channel_id=1, source_target_pairs={{0,4},{4,0},{1,5},{5,1},{2,6},{6,2},{3,7},{7,3},{8,12},{12,8},{9,1... | collective-permute-start | bytes 1769480 | tf_op jit(solution)/shard_map/ppermute | solution.py:22
  44.2 25.5 %collective-permute-start.6 = (bf16[256,1152]{1,0:T(8,128)(2,1)}, bf16[256,1152]{1,0:T(8,128)(2,1)}, u32[]{:S(2)}, u32[]{:S(2)}) collective-permute-start(bf16[256,1152]{1,0:T(8,128)(2,1)} %get-tuple-element.31), channel_id=1, source_target_pairs={{0,4},{4,0},{1,5},{5,1},{2,6},{6,2},{3,7},{7,3},{8,12},{12,8},{9,1... | collective-permute-start | bytes 1769480 | tf_op jit(solution)/shard_map/ppermute | solution.py:22
  49.8 29.8 %collective-permute-start.2 = (bf16[576,1152]{1,0:T(8,128)(2,1)}, bf16[576,1152]{1,0:T(8,128)(2,1)}, u32[]{:S(2)}, u32[]{:S(2)}) collective-permute-start(bf16[576,1152]{1,0:T(8,128)(2,1)} %fusion.5.refs_2_), channel_id=1, source_target_pairs={{0,1},{1,0},{2,3},{3,2},{4,5},{5,4},{6,7},{7,6},{8,9},{9,8},{10,11... | collective-permute-start | bytes 3981320 | tf_op jit(solution)/shard_map/ppermute | solution.py:22
  70.9 20.5 %copy-start.3 = (bf16[256,1152]{1,0:T(8,128)(2,1)}, bf16[256,1152]{1,0:T(8,128)(2,1)S(1)}, u32[]{:S(2)}) copy-start(bf16[256,1152]{1,0:T(8,128)(2,1)S(1)} %get-tuple-element.35.refs_6_) | copy-start | bytes 1769476
  70.9 20.5 %copy-start.5 = (bf16[256,1152]{1,0:T(8,128)(2,1)}, bf16[256,1152]{1,0:T(8,128)(2,1)S(1)}, u32[]{:S(2)}) copy-start(bf16[256,1152]{1,0:T(8,128)(2,1)S(1)} %get-tuple-element.34.refs_8_) | copy-start | bytes 1769476
  70.9 42.4 %collective-permute-start.10 = (bf16[256,1152]{1,0:T(8,128)(2,1)S(1)}, bf16[256,1152]{1,0:T(8,128)(2,1)S(1)}, u32[]{:S(2)}, u32[]{:S(2)}) collective-permute-start(bf16[256,1152]{1,0:T(8,128)(2,1)S(1)} %get-tuple-element.34.refs_8_), channel_id=1, source_target_pairs={{0,248},{8,0},{16,8},{24,16},{32,24},{40,32},{48,40},{56,48},{64,5... | collective-permute-start | bytes 1769480 | tf_op jit(solution)/shard_map/ppermute | solution.py:17
  77.2 14.1 %copy-start.4 = (bf16[256,1152]{1,0:T(8,128)(2,1)}, bf16[256,1152]{1,0:T(8,128)(2,1)S(1)}, u32[]{:S(2)}) copy-start(bf16[256,1152]{1,0:T(8,128)(2,1)S(1)} %get-tuple-element.33.refs_7_) | copy-start | bytes 1769476
  77.2 14.1 %copy-start.6 = (bf16[256,1152]{1,0:T(8,128)(2,1)}, bf16[256,1152]{1,0:T(8,128)(2,1)S(1)}, u32[]{:S(2)}) copy-start(bf16[256,1152]{1,0:T(8,128)(2,1)S(1)} %get-tuple-element.32.refs_9_) | copy-start | bytes 1769476
  77.2 36.1 %collective-permute-start.11 = (bf16[256,1152]{1,0:T(8,128)(2,1)S(1)}, bf16[256,1152]{1,0:T(8,128)(2,1)S(1)}, u32[]{:S(2)}, u32[]{:S(2)}) collective-permute-start(bf16[256,1152]{1,0:T(8,128)(2,1)S(1)} %get-tuple-element.32.refs_9_), channel_id=1, source_target_pairs={{0,248},{8,0},{16,8},{24,16},{32,24},{40,32},{48,40},{56,48},{64,5... | collective-permute-start | bytes 1769480 | tf_op jit(solution)/shard_map/ppermute | solution.py:17
  77.8 35.5 %collective-permute-start.7 = (bf16[256,1152]{1,0:T(8,128)(2,1)S(1)}, bf16[256,1152]{1,0:T(8,128)(2,1)S(1)}, u32[]{:S(2)}, u32[]{:S(2)}) collective-permute-start(bf16[256,1152]{1,0:T(8,128)(2,1)S(1)} %get-tuple-element.35.refs_6_), channel_id=1, source_target_pairs={{0,8},{8,16},{16,24},{24,32},{32,40},{40,48},{48,56},{56,64},{64,7... | collective-permute-start | bytes 1769480 | tf_op jit(solution)/shard_map/ppermute | solution.py:17
  79.5 33.8 %collective-permute-start.9 = (bf16[256,1152]{1,0:T(8,128)(2,1)S(1)}, bf16[256,1152]{1,0:T(8,128)(2,1)S(1)}, u32[]{:S(2)}, u32[]{:S(2)}) collective-permute-start(bf16[256,1152]{1,0:T(8,128)(2,1)S(1)} %get-tuple-element.33.refs_7_), channel_id=1, source_target_pairs={{0,8},{8,16},{16,24},{24,32},{32,40},{40,48},{48,56},{56,64},{64,7... | collective-permute-start | bytes 1769480 | tf_op jit(solution)/shard_map/ppermute | solution.py:17
  113.3 0.8 copy-start.10
  113.3 1.1 copy-start.11
  113.4 1.2 copy-start.12
  113.4 1.3 copy-start.13
  133.2 7.1 %collective-permute-start.12 = (bf16[16,96,896]{2,1,0:T(8,128)(2,1)}, bf16[16,96,896]{2,1,0:T(8,128)(2,1)S(1)}, u32[]{:S(2)}, u32[]{:S(2)}) collective-permute-start(bf16[16,96,896]{2,1,0:T(8,128)(2,1)} %get-tuple-element.25), channel_id=1, source_target_pairs={{0,1},{1,0},{2,3},{3,2},{4,5},{5,4},{6,7},{7,6},{8,9},{9,8},{10,11... | collective-permute-start | bytes 8257544 | tf_op jit(solution)/shard_map/ppermute | solution.py:22
  182.7 16.5 %copy-start.7 = (f32[288,36]{0,1:T(8,128)S(1)}, f32[288,36]{0,1:T(8,128)}, u32[]{:S(2)}) copy-start(f32[288,36]{0,1:T(8,128)} %param.13) | copy-start | bytes 124420
  182.7 16.5 %copy-start.8 = (f32[288,36]{0,1:T(8,128)S(1)}, f32[288,36]{0,1:T(8,128)}, u32[]{:S(2)}) copy-start(f32[288,36]{0,1:T(8,128)} %param.15) | copy-start | bytes 124420
  182.7 16.5 %copy-start.9 = (f32[288,36]{0,1:T(8,128)S(1)}, f32[288,36]{0,1:T(8,128)}, u32[]{:S(2)}) copy-start(f32[288,36]{0,1:T(8,128)} %param.14) | copy-start | bytes 124420
  213.9 20.0 %all-to-all-start.3 = ((bf16[8,96,896]{2,1,0:T(8,128)(2,1)}), bf16[8,96,896]{2,1,0:T(8,128)(2,1)S(1)}, u32[]{:S(2)}, u32[]{:S(2)}) async-start(bf16[8,96,896]{2,1,0:T(8,128)(2,1)} %broadcast_in_dim.21), calls=%async_computation.3 | async-start | bytes 2752512 | tf_op jit(solution)/shard_map/all_to_all | solution.py:394
  217.7 4.4 %copy-start.2 = (bf16[2,512,1152]{2,1,0:T(8,128)(2,1)S(1)}, bf16[2,512,1152]{2,1,0:T(8,128)(2,1)}, u32[]{:S(2)}) copy-start(bf16[2,512,1152]{2,1,0:T(8,128)(2,1)} %get-tuple-element.24.in_tan) | copy-start | bytes 7077892

commit v3 on v2

--- a/solution.py
+++ b/solution.py
@@ -35,18 +35,17 @@
 
 def exchange(img, txt):
     even = lax.axis_index("xl") == 0
-    two_t = shifted(txt, 1)
-    two_i = shifted(img, -1)
+    piece = txt.shape[0] // PIECES
+    cuts = [slice(n * piece, (n + 1) * piece) for n in range(PIECES)]
     first = swapped(jnp.where(even, txt, img), "xl")
-    one_t, one_i, three_t, three_i = [], [], [], []
-    piece = txt.shape[0] // PIECES
-    seconds = []
+    two_t = [shifted(txt[cut], 1) for cut in cuts]
+    two_i = [shifted(img[cut], -1) for cut in cuts]
+    one_t, one_i, three_t, three_i, seconds = [], [], [], [], []
     for n in range(PIECES):
-        cut = slice(n * piece, (n + 1) * piece)
-        held = jnp.where(even, two_i[cut], two_t[cut])
+        at_t, at_i = lax.optimization_barrier((two_t[n], two_i[n]))
+        held = jnp.where(even, at_i, at_t)
         seconds.append(swapped(held, "xl"))
-    for n in range(PIECES):
-        cut = slice(n * piece, (n + 1) * piece)
+    for n, cut in enumerate(cuts):
         near, far = lax.optimization_barrier((first, seconds[n]))
         one_t.append(jnp.where(even, far, near[cut]))
         one_i.append(jnp.where(even, near[cut], far))
@@ -160,16 +159,16 @@
 
 
 def meet_kernel(mult_ref, offset_ref, tops, *refs):
-    shards, (two_t, two_i), refs = refs[:4], refs[4:6], refs[6:]
-    texts, images, refs = refs[:PIECES], refs[PIECES : 2 * PIECES], refs[2 * PIECES :]
-    in_low, in_acc, acc, w, raw, low, sems = refs
+    shards, refs = refs[:4], refs[4:]
+    two_t, two_i, texts, images = (refs[n * PIECES : (n + 1) * PIECES] for n in range(4))
+    in_low, in_acc, acc, w, raw, low, sems = refs[4 * PIECES :]
     mult, offset = mult_ref[0], offset_ref[0]
     loads = Loads(sems)
     ready = []
     for side, two in enumerate((two_t, two_i)):
         ready.append(
             load_weights(loads, tops, shards, w, 1 - side)
-            + load_rows(loads, [two], raw.at[side])
+            + load_rows(loads, two, raw.at[side])
             + [loads.plan(in_low.at[side], low.at[side])]
             + [loads.plan(in_acc.at[side], acc.at[side])]
         )
@@ -347,7 +346,7 @@
     (acc,) = call(
         meet_kernel,
         (big,),
-        (*scalars, *shards, two_t, two_i, *one_t, *one_i, low_of, acc),
+        (*scalars, *shards, *two_t, *two_i, *one_t, *one_i, low_of, acc),
         mac * (4 * WIDTH + 8 * ROWS),
         scalars=3,
         scratch=(vw, pltpu.VMEM((4, ROWS, WIDTH), bf16), vlow),

time: 239 us -> 248 us (1.038)
  starting transfers between devices: 23.5 us -> 28.6 us
  local copies, waits for them, and re-layouts: 5.74 us -> 9.14 us
    ppermute x7, waiting for transfers between devices: 15.4 us -> 29.1 us  [swapped(): return lax.ppermute(value, axes, [(i, count - 1 - i) for i in range(count)])]
    ppermute x6 -> x8, waiting for transfers between devices: 23.8 us -> 10.7 us  [shifted(): lax.ppermute(value, LINE, [(i, (i + steps) % count) for i in range(count)])]
    ppermute x6 -> x8, starting transfers between devices: 15.8 us -> 21.2 us  [shifted(): lax.ppermute(value, LINE, [(i, (i + steps) % count) for i in range(count)])]
    slice x0 -> x2, local copies, waits for them, and re-layouts: none -> 3.27 us  [the longest x1 2.37 us: exchange(): two_t = [shifted(txt[cut], 1) for cut in cuts]]
  transfers between devices with their start and end apart: 14 -> 16, of which waited for: 5 -> 5; matrix products, arithmetic and copies ran while one was open for 11% -> 12% of each run, Pallas kernels for 17% -> 16%
where the time goes in v3:
time: 248 us; the launch traced here: 247 us
  blocking collectives  66.6 us (27%)
  Pallas kernels  63.1 us (25%)
  waiting for transfers between devices  48.5 us (20%)
  starting transfers between devices  28.6 us (12%)
  other arithmetic  14.7 us (6%)
  matrix products  14 us (6%)
  local copies, waits for them, and re-layouts  9.14 us (4%)
    pallas_call x5, Pallas kernels, call(): pl.pallas_call(kernel, out_shape=outs, in_specs=[SMEM] * scalars + [spec]...  63.1 us
    all_to_all x1, blocking collectives, inner(): parts = lax.all_to_all(chip, ('y', 'xl', 'xh'), 0, 0, tiled=True)  39.7 us
    ppermute x7, waiting for transfers between devices, swapped(): return lax.ppermute(value, axes, [(i, count - 1 - i) for i in range(count)])  29.1 us
    ppermute x8, starting transfers between devices, shifted(): lax.ppermute(value, LINE, [(i, (i + steps) % count) for i in range(count)])  21.2 us
    all_to_all x1, blocking collectives, inner(): parts = lax.all_to_all(plane.reshape(8, 12, LANES), 'z', 0, 0, tiled=True)  14.3 us
    dot_general x4, matrix products, dot(): lax.dot_general(left, right, (dims, ((), ())), preferred_element_type=jnp...  14 us
    all_to_all x1, blocking collectives, inner(): lax.all_to_all(jnp.broadcast_to(mine, (8, 12, LANES)), 'z', 0, 0, tiled=T...  12.5 us
    ppermute x8, waiting for transfers between devices, shifted(): lax.ppermute(value, LINE, [(i, (i + steps) % count) for i in range(count)])  10.7 us
  transfers between devices with their start and end apart: 16, of which 5 were waited for; matrix products, arithmetic and copies ran while one was open for 12% of the time, Pallas kernels for 16%

profile of v3, /device:TPU:4, one launch (start us, length us, event | category | flops | bytes accessed | tf_op | source)
XLA Modules:
  0.0 246.9 jit_solution(18013851646176683763)
XLA Ops:
  1.3 2.4 fusion.117
  3.6 1.9 collective-permute-start.8
  6.5 6.4 %collective-permute-start.9 = (bf16[256,1152]{1,0:T(8,128)(2,1)S(1)}, bf16[256,1152]{1,0:T(8,128)(2,1)}, u32[]{:S(2)}, u32[]{:S(2)}) collective-permute-start(bf16[256,1152]{1,0:T(8,128)(2,1)S(1)} %get-tuple-element.54), channel_id=1, source_target_pairs={{0,248},{8,0},{16,8},{24,16},{32,24},{40,32},{48,40},{56,48},{64,5... | collective-permute-start | bytes 1769480 | tf_op jit(solution)/shard_map/ppermute | solution.py:17
  12.9 5.3 %collective-permute-start.5 = (bf16[256,1152]{1,0:T(8,128)(2,1)}, bf16[256,1152]{1,0:T(8,128)(2,1)}, u32[]{:S(2)}, u32[]{:S(2)}) collective-permute-start(bf16[256,1152]{1,0:T(8,128)(2,1)} %get-tuple-element.55), channel_id=1, source_target_pairs={{0,248},{8,0},{16,8},{24,16},{32,24},{40,32},{48,40},{56,48},{64,5... | collective-permute-start | bytes 1769480 | tf_op jit(solution)/shard_map/ppermute | solution.py:17
  20.1 3.3 %fusion.4.refs_0_ = bf16[576,1152]{1,0:T(8,128)(2,1)} fusion(s32[1152]{0:T(1024)S(1)} %fusion.60, bf16[288,1152]{1,0:T(8,128)(2,1)S(1)} %get-tuple-element.45, bf16[288,1152]{1,0:T(8,128)(2,1)S(1)} %get-tuple-element.44), kind=kOutput, calls=%fused_computation.6 | convolution fusion | flops 1533468672 | bytes 2658816 | tf_op jit(solution)/shard_map/dot_general | solution.py:69
  23.4 2.9 %collective-permute-done.8.refs_5_ = bf16[256,1152]{1,0:T(8,128)(2,1)S(1)} collective-permute-done((bf16[256,1152]{1,0:T(8,128)(2,1)}, bf16[256,1152]{1,0:T(8,128)(2,1)S(1)}, u32[]{:S(2)}, u32[]{:S(2)}) %collective-permute-start.8) | collective-permute-done | bytes 589856 | tf_op jit(solution)/shard_map/ppermute | solution.py:17
  28.3 2.0 broadcast_select_fusion.4
  30.3 7.7 %collective-permute-done.4.refs_4_ = bf16[256,1152]{1,0:T(8,128)(2,1)} collective-permute-done((bf16[256,1152]{1,0:T(8,128)(2,1)}, bf16[256,1152]{1,0:T(8,128)(2,1)}, u32[]{:S(2)}, u32[]{:S(2)}) %collective-permute-start.4) | collective-permute-done | bytes 589856 | tf_op jit(solution)/shard_map/ppermute | solution.py:17
  39.1 1.9 broadcast_select_fusion.6
  42.0 1.4 fusion.114
  43.3 3.3 %fusion.5.refs_2_ = bf16[576,1152]{1,0:T(8,128)(2,1)} fusion(s32[1152]{0:T(1024)S(1)} %fusion.60, bf16[288,1152]{1,0:T(8,128)(2,1)S(1)} %get-tuple-element.43, bf16[288,1152]{1,0:T(8,128)(2,1)S(1)} %get-tuple-element.42), kind=kOutput, calls=%fused_computation.7 | convolution fusion | flops 1533468672 | bytes 2658816 | tf_op jit(solution)/shard_map/dot_general | solution.py:69
  46.6 2.7 %broadcast_select_fusion.7 = (bf16[512,288]{1,0:T(8,128)(2,1)}, bf16[512,288]{1,0:T(8,128)(2,1)}, bf16[512,288]{1,0:T(8,128)(2,1)}, bf16[512,288]{1,0:T(8,128)(2...) fusion(pred[]{:T(512)S(6)} %eq.74, ...), kind=kLoop, calls=%fused_computation.34 | loop fusion | flops 1179648 | bytes 4718594 | tf_op jit(solution)/shard_map/jit(_where)/select_n | solution.py:324
  51.3 17.7 %collective-permute-done.10 = bf16[256,1152]{1,0:T(8,128)(2,1)} collective-permute-done((bf16[256,1152]{1,0:T(8,128)(2,1)}, bf16[256,1152]{1,0:T(8,128)(2,1)}, u32[]{:S(2)}, u32[]{:S(2)}) %collective-permute-start.10) | collective-permute-done | bytes 589856 | tf_op jit(solution)/shard_map/ppermute | solution.py:22
  68.9 11.4 %collective-permute-done.6 = bf16[256,1152]{1,0:T(8,128)(2,1)} collective-permute-done((bf16[256,1152]{1,0:T(8,128)(2,1)}, bf16[256,1152]{1,0:T(8,128)(2,1)}, u32[]{:S(2)}, u32[]{:S(2)}) %collective-permute-start.6) | collective-permute-done | bytes 589856 | tf_op jit(solution)/shard_map/ppermute | solution.py:22
  80.3 1.2 broadcast_select_fusion.1
  81.6 5.3 %collective-permute-start.13 = (bf16[256,1152]{1,0:T(8,128)(2,1)S(1)}, bf16[256,1152]{1,0:T(8,128)(2,1)S(1)}, u32[]{:S(2)}, u32[]{:S(2)}) collective-permute-start(bf16[256,1152]{1,0:T(8,128)(2,1)S(1)} %get-tuple-element.38.refs_11_), channel_id=1, source_target_pairs={{0,248},{8,0},{16,8},{24,16},{32,24},{40,32},{48,40},{56,48},{64,5... | collective-permute-start | bytes 1769480 | tf_op jit(solution)/shard_map/ppermute | solution.py:17
  87.0 1.2 broadcast_select_fusion.2
  88.3 2.0 collective-permute-start.7
  90.3 11.8 %shard_map.127 = (f32[2,512,1152]{2,1,0:T(8,128)}, f32[2,512,1]{2,1,0:T(8,128)}, bf16[2,512,1152]{2,1,0:T(8,128)(2,1)}, f32[2,512,1152]{2,1,0:T(8,128)}) custom-call(f32[1]{0:T(128)S(6)} %copy.19.mult_ref, f32[1]{0:T(128)S(6)} %copy.20.offset_ref, s32[4]{0:T(128)} %add_multiply_fusion.tops, bf16[576,1152]{1,0:T(8,128)(2,1)} %fusion.4.refs_0_, ...), custom_call_target="tpu_custom_call" | custom-call | flops 4529848320 | bytes 19468312 | tf_op jit(solution)/shard_map/pallas_call | solution.py:276
  102.1 22.0 %shard_map.128.refs_9_ = f32[2,512,1152]{2,1,0:T(8,128)} custom-call(f32[1]{0:T(128)S(6)} %copy.19.mult_ref, f32[1]{0:T(128)S(6)} %copy.20.offset_ref, s32[4]{0:T(128)} %add_multiply_fusion.tops, bf16[576,1152]{1,0:T(8,128)(2,1)} %fusion.4.refs_0_, bf16[576,1152]{1,0:T(8,128)(2,1)} %collective-permute-done.refs_1_, bf16[576,1152]{1,0:T(8,128)(2,1)} %fusion.5.refs_2_, ...), custom_call_target="tpu_custom_call" | custom-call | flops 10267656192 | bytes 21823512 | tf_op jit(solution)/shard_map/pallas_call | solution.py:276
  125.5 18.5 %shard_map.129 = (bf16[2,512,1152]{2,1,0:T(8,128)(2,1)}, bf16[16,96,896]{2,1,0:T(8,128)(2,1)}) custom-call(f32[1]{0:T(128)S(6)} %copy.19.mult_ref, f32[1]{0:T(128)S(6)} %copy.20.offset_ref, s32[4]{0:T(128)} %add_multiply_fusion.tops, bf16[576,1152]{1,0:T(8,128)(2,1)} %fusion.4.refs_0_, bf16[576,1152]{1,0:T(8,128)(2,1)} %collective-permute-done.refs_1_, ...), custom_call_target="tpu_custom_call" | custom-call | flops 6492782592 | bytes 25759768 | tf_op jit(solution)/shard_map/pallas_call | solution.py:276
  144.2 6.8 %shard_map.130 = bf16[16,96,896]{2,1,0:T(8,128)(2,1)} custom-call(bf16[2,512,1152]{2,1,0:T(8,128)(2,1)} %get-tuple-element.32.in_tan, bf16[512,288]{1,0:T(8,128)(2,1)} %get-tuple-element.58.refs_0_, bf16[512,288]{1,0:T(8,128)(2,1)} %get-tuple-element.61.refs_1_, bf16[512,288]{1,0:T(8,128)(2,1)} %get-tuple-element.49.refs_2_, ...), custom_call_target="tpu_custom_call" | custom-call | flops 1358954496 | bytes 6291456 | tf_op jit(solution)/shard_map/pallas_call | solution.py:276
  151.0 2.5 add_convert_fusion
  153.4 39.7 %all_to_all.20 = bf16[16,96,896]{2,1,0:T(8,128)(2,1)S(1)} all-to-all(bf16[16,96,896]{2,1,0:T(8,128)(2,1)S(1)} %add_convert_fusion), channel_id=1, replica_groups=mesh['y'=4,'z'=8,'xl'=2,'xh'=2,'c'=2] {'y','xl','xh'}, dimensions={0} | all-to-all | bytes 5505024 | tf_op jit(solution)/shard_map/all_to_all | solution.py:378
  193.7 14.3 %all_to_all.21 = bf16[8,12,896]{2,1,0:T(8,128)(2,1)S(1)} all-to-all(bf16[8,12,896]{2,1,0:T(8,128)(2,1)S(1)} %reshape.167), channel_id=1, replica_groups=mesh['y'=4,'z'=8,'xl'=2,'xh'=2,'c'=2] {'z'}, dimensions={0} | all-to-all | bytes 344064 | tf_op jit(solution)/shard_map/all_to_all | solution.py:380
  209.1 12.5 %all_to_all.22 = bf16[8,12,896]{2,1,0:T(8,128)(2,1)S(1)} all-to-all(bf16[8,12,896]{2,1,0:T(8,128)(2,1)S(1)} %broadcast_in_dim.9), channel_id=1, replica_groups=mesh['y'=4,'z'=8,'xl'=2,'xh'=2,'c'=2] {'z'}, dimensions={0} | all-to-all | bytes 344064 | tf_op jit(solution)/shard_map/all_to_all | solution.py:391
  221.6 1.2 broadcast_in_dim.21
  222.9 3.6 %all-to-all-start.3 = ((bf16[8,96,896]{2,1,0:T(8,128)(2,1)}), bf16[8,96,896]{2,1,0:T(8,128)(2,1)S(1)}, u32[]{:S(2)}, u32[]{:S(2)}) async-start(bf16[8,96,896]{2,1,0:T(8,128)(2,1)} %broadcast_in_dim.21), calls=%async_computation.3 | async-start | bytes 2752512 | tf_op jit(solution)/shard_map/all_to_all | solution.py:393
  226.7 4.4 %fusion.7 = bf16[512,1152]{1,0:T(8,128)(2,1)} fusion(s32[1152]{0:T(1024)S(1)} %fusion.60, bf16[2,512,1152]{2,1,0:T(8,128)(2,1)} %get-tuple-element.32.in_tan), kind=kOutput, calls=%fused_computation.9 | convolution fusion | flops 1360871424 | bytes 2363904 | tf_op jit(solution)/shard_map/dot_general | solution.py:69
  231.1 3.0 %fusion.6 = bf16[512,1152]{1,0:T(8,128)(2,1)} fusion(s32[1152]{0:T(1024)S(1)} %fusion.60, bf16[2,512,1152]{2,1,0:T(8,128)(2,1)S(1)} %copy-done.2), kind=kOutput, calls=%fused_computation.8 | convolution fusion | flops 1360871424 | bytes 2367488 | tf_op jit(solution)/shard_map/dot_general | solution.py:69
  234.1 8.7 %all-to-all-done.3.parts = bf16[8,96,896]{2,1,0:T(8,128)(2,1)S(1)} async-done(((bf16[8,96,896]{2,1,0:T(8,128)(2,1)}), bf16[8,96,896]{2,1,0:T(8,128)(2,1)S(1)}, u32[]{:S(2)}, u32[]{:S(2)}) %all-to-all-start.3) | async-done | bytes 1376288 | tf_op jit(solution)/shard_map/all_to_all | solution.py:393
  242.9 4.1 %shard_map.131 = bf16[288,2304]{1,0:T(8,128)(2,1)} custom-call(bf16[8,96,896]{2,1,0:T(8,128)(2,1)S(1)} %all-to-all-done.3.parts, bf16[576,576]{1,0:T(8,128)(2,1)S(1)} %fusion.12.order), custom_call_target="tpu_custom_call" | custom-call | flops 764411904 | bytes 3366912 | tf_op jit(solution)/shard_map/pallas_call | solution.py:276
  (73 shorter events, 11.4 us)
Async XLA Ops:
  0.6 4.9 %copy-start = (bf16[512,1152]{1,0:T(8,128)(2,1)S(1)}, bf16[512,1152]{1,0:T(8,128)(2,1)}, u32[]{:S(2)}) copy-start(bf16[512,1152]{1,0:T(8,128)(2,1)} %refs_4_.1) | copy-start | bytes 3538948
  0.6 41.3 %collective-permute-start.1 = (bf16[288,2304]{1,0:T(8,128)(2,1)}, bf16[288,2304]{1,0:T(8,128)(2,1)}, u32[]{:S(2)}, u32[]{:S(2)}) collective-permute-start(bf16[288,2304]{1,0:T(8,128)(2,1)} %param.10), channel_id=1, source_target_pairs={{0,6},{2,4},{4,2},{6,0},{1,7},{3,5},{5,3},{7,1},{8,14},{10,12},{12... | collective-permute-start | bytes 3981320 | tf_op jit(solution)/shard_map/ppermute | solution.py:22
  3.6 14.6 %copy-start.1 = (bf16[512,1152]{1,0:T(8,128)(2,1)S(1)}, bf16[512,1152]{1,0:T(8,128)(2,1)}, u32[]{:S(2)}) copy-start(bf16[512,1152]{1,0:T(8,128)(2,1)} %refs_5_.1) | copy-start | bytes 3538948
  3.6 22.7 %collective-permute-start.8 = (bf16[256,1152]{1,0:T(8,128)(2,1)}, bf16[256,1152]{1,0:T(8,128)(2,1)S(1)}, u32[]{:S(2)}, u32[]{:S(2)}) collective-permute-start(bf16[256,1152]{1,0:T(8,128)(2,1)} %get-tuple-element.56), channel_id=1, source_target_pairs={{0,8},{8,16},{16,24},{24,32},{32,40},{40,48},{48,56},{56,64},{64,7... | collective-permute-start | bytes 1769480 | tf_op jit(solution)/shard_map/ppermute | solution.py:17
  6.5 20.7 %collective-permute-start.9 = (bf16[256,1152]{1,0:T(8,128)(2,1)S(1)}, bf16[256,1152]{1,0:T(8,128)(2,1)}, u32[]{:S(2)}, u32[]{:S(2)}) collective-permute-start(bf16[256,1152]{1,0:T(8,128)(2,1)S(1)} %get-tuple-element.54), channel_id=1, source_target_pairs={{0,248},{8,0},{16,8},{24,16},{32,24},{40,32},{48,40},{56,48},{64,5... | collective-permute-start | bytes 1769480 | tf_op jit(solution)/shard_map/ppermute | solution.py:17
  12.9 25.1 %collective-permute-start.4 = (bf16[256,1152]{1,0:T(8,128)(2,1)}, bf16[256,1152]{1,0:T(8,128)(2,1)}, u32[]{:S(2)}, u32[]{:S(2)}) collective-permute-start(bf16[256,1152]{1,0:T(8,128)(2,1)} %get-tuple-element.57), channel_id=1, source_target_pairs={{0,8},{8,16},{16,24},{24,32},{32,40},{40,48},{48,56},{56,64},{64,7... | collective-permute-start | bytes 1769480 | tf_op jit(solution)/shard_map/ppermute | solution.py:17
  12.9 26.3 %collective-permute-start.5 = (bf16[256,1152]{1,0:T(8,128)(2,1)}, bf16[256,1152]{1,0:T(8,128)(2,1)}, u32[]{:S(2)}, u32[]{:S(2)}) collective-permute-start(bf16[256,1152]{1,0:T(8,128)(2,1)} %get-tuple-element.55), channel_id=1, source_target_pairs={{0,248},{8,0},{16,8},{24,16},{32,24},{40,32},{48,40},{56,48},{64,5... | collective-permute-start | bytes 1769480 | tf_op jit(solution)/shard_map/ppermute | solution.py:17
  18.2 1.7 copy-start.3
  26.3 0.8 copy-start.8
  26.3 62.0 %collective-permute-start = (bf16[576,1152]{1,0:T(8,128)(2,1)}, bf16[576,1152]{1,0:T(8,128)(2,1)}, u32[]{:S(2)}, u32[]{:S(2)}) collective-permute-start(bf16[576,1152]{1,0:T(8,128)(2,1)} %fusion.4.refs_0_), channel_id=1, source_target_pairs={{0,1},{1,0},{2,3},{3,2},{4,5},{5,4},{6,7},{7,6},{8,9},{9,8},{10,11... | collective-permute-start | bytes 3981320 | tf_op jit(solution)/shard_map/ppermute | solution.py:22
  27.1 41.8 %collective-permute-start.3 = (bf16[512,1152]{1,0:T(8,128)(2,1)}, bf16[512,1152]{1,0:T(8,128)(2,1)S(1)}, u32[]{:S(2)}, u32[]{:S(2)}) collective-permute-start(bf16[512,1152]{1,0:T(8,128)(2,1)} %broadcast_select_fusion), channel_id=1, source_target_pairs={{0,4},{4,0},{1,5},{5,1},{2,6},{6,2},{3,7},{7,3},{8,12},{12,8},{9,1... | collective-permute-start | bytes 3538952 | tf_op jit(solution)/shard_map/ppermute | solution.py:22
  38.0 31.0 %collective-permute-start.10 = (bf16[256,1152]{1,0:T(8,128)(2,1)}, bf16[256,1152]{1,0:T(8,128)(2,1)}, u32[]{:S(2)}, u32[]{:S(2)}) collective-permute-start(bf16[256,1152]{1,0:T(8,128)(2,1)} %broadcast_select_fusion.4), channel_id=1, source_target_pairs={{0,4},{4,0},{1,5},{5,1},{2,6},{6,2},{3,7},{7,3},{8,12},{12,8},{9,1... | collective-permute-start | bytes 1769480 | tf_op jit(solution)/shard_map/ppermute | solution.py:22
  41.1 39.2 %collective-permute-start.6 = (bf16[256,1152]{1,0:T(8,128)(2,1)}, bf16[256,1152]{1,0:T(8,128)(2,1)}, u32[]{:S(2)}, u32[]{:S(2)}) collective-permute-start(bf16[256,1152]{1,0:T(8,128)(2,1)} %broadcast_select_fusion.6), channel_id=1, source_target_pairs={{0,4},{4,0},{1,5},{5,1},{2,6},{6,2},{3,7},{7,3},{8,12},{12,8},{9,1... | collective-permute-start | bytes 1769480 | tf_op jit(solution)/shard_map/ppermute | solution.py:22
  46.6 43.7 %collective-permute-start.2 = (bf16[576,1152]{1,0:T(8,128)(2,1)}, bf16[576,1152]{1,0:T(8,128)(2,1)}, u32[]{:S(2)}, u32[]{:S(2)}) collective-permute-start(bf16[576,1152]{1,0:T(8,128)(2,1)} %fusion.5.refs_2_), channel_id=1, source_target_pairs={{0,1},{1,0},{2,3},{3,2},{4,5},{5,4},{6,7},{7,6},{8,9},{9,8},{10,11... | collective-permute-start | bytes 3981320 | tf_op jit(solution)/shard_map/ppermute | solution.py:22
  81.5 20.6 %copy-start.4 = (bf16[256,1152]{1,0:T(8,128)(2,1)}, bf16[256,1152]{1,0:T(8,128)(2,1)S(1)}, u32[]{:S(2)}) copy-start(bf16[256,1152]{1,0:T(8,128)(2,1)S(1)} %get-tuple-element.38.refs_11_) | copy-start | bytes 1769476
  81.5 20.6 %copy-start.5 = (bf16[256,1152]{1,0:T(8,128)(2,1)}, bf16[256,1152]{1,0:T(8,128)(2,1)S(1)}, u32[]{:S(2)}) copy-start(bf16[256,1152]{1,0:T(8,128)(2,1)S(1)} %get-tuple-element.39.refs_9_) | copy-start | bytes 1769476
  81.5 42.6 %collective-permute-start.11 = (bf16[256,1152]{1,0:T(8,128)(2,1)S(1)}, bf16[256,1152]{1,0:T(8,128)(2,1)S(1)}, u32[]{:S(2)}, u32[]{:S(2)}) collective-permute-start(bf16[256,1152]{1,0:T(8,128)(2,1)S(1)} %get-tuple-element.39.refs_9_), channel_id=1, source_target_pairs={{0,8},{8,16},{16,24},{24,32},{32,40},{40,48},{48,56},{56,64},{64,7... | collective-permute-start | bytes 1769480 | tf_op jit(solution)/shard_map/ppermute | solution.py:17
  81.6 42.5 %collective-permute-start.13 = (bf16[256,1152]{1,0:T(8,128)(2,1)S(1)}, bf16[256,1152]{1,0:T(8,128)(2,1)S(1)}, u32[]{:S(2)}, u32[]{:S(2)}) collective-permute-start(bf16[256,1152]{1,0:T(8,128)(2,1)S(1)} %get-tuple-element.38.refs_11_), channel_id=1, source_target_pairs={{0,248},{8,0},{16,8},{24,16},{32,24},{40,32},{48,40},{56,48},{64,5... | collective-permute-start | bytes 1769480 | tf_op jit(solution)/shard_map/ppermute | solution.py:17
  88.2 13.9 %copy-start.6 = (bf16[256,1152]{1,0:T(8,128)(2,1)}, bf16[256,1152]{1,0:T(8,128)(2,1)S(1)}, u32[]{:S(2)}) copy-start(bf16[256,1152]{1,0:T(8,128)(2,1)S(1)} %get-tuple-element.41.refs_8_) | copy-start | bytes 1769476
  88.2 13.9 %copy-start.7 = (bf16[256,1152]{1,0:T(8,128)(2,1)}, bf16[256,1152]{1,0:T(8,128)(2,1)S(1)}, u32[]{:S(2)}) copy-start(bf16[256,1152]{1,0:T(8,128)(2,1)S(1)} %get-tuple-element.40.refs_10_) | copy-start | bytes 1769476
  88.2 36.0 %collective-permute-start.12 = (bf16[256,1152]{1,0:T(8,128)(2,1)S(1)}, bf16[256,1152]{1,0:T(8,128)(2,1)S(1)}, u32[]{:S(2)}, u32[]{:S(2)}) collective-permute-start(bf16[256,1152]{1,0:T(8,128)(2,1)S(1)} %get-tuple-element.40.refs_10_), channel_id=1, source_target_pairs={{0,248},{8,0},{16,8},{24,16},{32,24},{40,32},{48,40},{56,48},{64,5... | collective-permute-start | bytes 1769480 | tf_op jit(solution)/shard_map/ppermute | solution.py:17
  88.3 35.9 %collective-permute-start.7 = (bf16[256,1152]{1,0:T(8,128)(2,1)S(1)}, bf16[256,1152]{1,0:T(8,128)(2,1)S(1)}, u32[]{:S(2)}, u32[]{:S(2)}) collective-permute-start(bf16[256,1152]{1,0:T(8,128)(2,1)S(1)} %get-tuple-element.41.refs_8_), channel_id=1, source_target_pairs={{0,8},{8,16},{16,24},{24,32},{32,40},{40,48},{48,56},{56,64},{64,7... | collective-permute-start | bytes 1769480 | tf_op jit(solution)/shard_map/ppermute | solution.py:17
  124.1 0.8 copy-start.12
  124.2 1.0 copy-start.13
  124.2 1.2 copy-start.14
  124.2 1.3 copy-start.15
  144.1 6.9 %collective-permute-start.14 = (bf16[16,96,896]{2,1,0:T(8,128)(2,1)}, bf16[16,96,896]{2,1,0:T(8,128)(2,1)S(1)}, u32[]{:S(2)}, u32[]{:S(2)}) collective-permute-start(bf16[16,96,896]{2,1,0:T(8,128)(2,1)} %get-tuple-element.33), channel_id=1, source_target_pairs={{0,1},{1,0},{2,3},{3,2},{4,5},{5,4},{6,7},{7,6},{8,9},{9,8},{10,11... | collective-permute-start | bytes 8257544 | tf_op jit(solution)/shard_map/ppermute | solution.py:22
  193.6 14.6 %copy-start.9 = (f32[288,36]{0,1:T(8,128)S(1)}, f32[288,36]{0,1:T(8,128)}, u32[]{:S(2)}) copy-start(f32[288,36]{0,1:T(8,128)} %param.13) | copy-start | bytes 124420
  193.6 14.6 %copy-start.10 = (f32[288,36]{0,1:T(8,128)S(1)}, f32[288,36]{0,1:T(8,128)}, u32[]{:S(2)}) copy-start(f32[288,36]{0,1:T(8,128)} %param.15) | copy-start | bytes 124420
  193.6 14.6 %copy-start.11 = (f32[288,36]{0,1:T(8,128)S(1)}, f32[288,36]{0,1:T(8,128)}, u32[]{:S(2)}) copy-start(f32[288,36]{0,1:T(8,128)} %param.14) | copy-start | bytes 124420
  222.9 20.0 %all-to-all-start.3 = ((bf16[8,96,896]{2,1,0:T(8,128)(2,1)}), bf16[8,96,896]{2,1,0:T(8,128)(2,1)S(1)}, u32[]{:S(2)}, u32[]{:S(2)}) async-start(bf16[8,96,896]{2,1,0:T(8,128)(2,1)} %broadcast_in_dim.21), calls=%async_computation.3 | async-start | bytes 2752512 | tf_op jit(solution)/shard_map/all_to_all | solution.py:393
  226.7 4.4 %copy-start.2 = (bf16[2,512,1152]{2,1,0:T(8,128)(2,1)S(1)}, bf16[2,512,1152]{2,1,0:T(8,128)(2,1)}, u32[]{:S(2)}) copy-start(bf16[2,512,1152]{2,1,0:T(8,128)(2,1)} %get-tuple-element.32.in_tan) | copy-start | bytes 7077892
